TPU v7x, 128 devices: a whole 4x4x4 slice. The times are simulated.
128 devices in a mesh: dp: 4 (over y), expert: 32 (over x, z, core).
Axes of the slice: x: 4, y: 4, z: 4, core: 2. Of those that a mesh axis runs over, the one named last changes fastest.
Arguments:
- hidden_in: bfloat16 [32768, 1024], P(('dp', 'expert')), may hold values from -6 to 6
- moe_gain: float32 [1024], replicated, may hold values from 0.1 to 1.9
- router_weight: bfloat16 [1024, 64], replicated, may hold values from -0.1875 to 0.1875
- expert_gate: bfloat16 [64, 1024, 1024], P('expert'), may hold values from -0.1875 to 0.1875
- expert_up: bfloat16 [64, 1024, 1024], P('expert'), may hold values from -0.1875 to 0.1875
- expert_down: bfloat16 [64, 1024, 1024], P('expert'), may hold values from -0.1875 to 0.1875
- final_gain: float32 [1024], replicated, may hold values from 0.1 to 1.9
- vocab_weight: bfloat16 [1024, 32768], P(None, 'expert'), may hold values from -24 to 24
- token_ids: int32 [32768], P(('dp', 'expert')), may hold values from 0 to 32767
- doc_ids: int32 [32768], P(('dp', 'expert')), may hold values from 0 to 511, as said below
- routes: int32 [32768, 2], P(('dp', 'expert')), may hold values from 0 to 63, all different within a row; in each aligned block of 256 rows (0 to 255, 256 to 511, ...) at most 16 rows name the same one
Outputs:
- token_loss: float32 [32768], P(('dp', 'expert'))
- doc_score: float32 [512], P(('dp', 'expert'))
Inputs may be any that keep to these rules, and one draw needn't show every extreme that they name: `routes`: among the rows of one device no expert is named more than 16 times; in every draw some expert is named exactly 16 times by the rows of some device. `doc_ids`: documents are numbered in the order of the stream; each document is one run of consecutive tokens, shorter than 512; every document number is used; the rows of each device hold the first tokens of exactly 4 documents.
All inputs are finite; a program needn't handle non-finite values.
Results may differ from a plain program's by a relative error of at most 0.0031.
Values may be sent and summed in bfloat16 or wider, within the bound.
A program may use at most 128 MiB of HBM per device.

v0:
```python
import jax
import jax.numpy as jnp
from jax import lax
from jax.sharding import Mesh
from jax.sharding import PartitionSpec as P

TOP = 2
DOC_DEV = 4
EXPERT = ("expert_0", "expert_1", "expert_2")
DP_EXPERT = ("dp", "expert_0", "expert_1", "expert_2")


EPSILON = 1e-06


def shifted(value, axis, steps):
    count = lax.axis_size(axis)
    first, last = (max(0, -steps), min(count, count - steps))
    return lax.ppermute(value, axis, [(source, source + steps) for source in range(first, last)])


def gathered_once(value, axis):
    leaves = jax.tree.leaves(value)
    sequence = sorted(range(len(leaves)), key=lambda k: -leaves[k].size)
    width = (1, *leaves[sequence[0]].shape)[-1]
    lines = [
        jnp.pad(leaves[k].reshape(-1), (0, -leaves[k].size % width)).reshape(-1, width)
        for k in sequence
    ]
    both, at, found = (lax.all_gather(jnp.concatenate(lines), axis), 0, {})
    for k, line in zip(sequence, lines):
        slab = both[:, at : at + len(line)].reshape(len(both), -1)
        found[k] = slab[:, : leaves[k].size].reshape(-1, *leaves[k].shape)
        at += len(line)
    numbers = iter(range(len(leaves)))
    return jax.tree.map(lambda _: found[next(numbers)], value)


def merged_by_axis(value, axes, combine):
    for axis in axes:
        pieces = gathered_once(value, axis)
        value = jax.tree.map(lambda part: part[0], pieces)
        for k in range(1, lax.axis_size(axis)):
            value = combine(value, jax.tree.map(lambda part: part[k], pieces))
    return value


def by_axis(value, axes):
    for axis in axes:
        value = lax.psum(value, axis)
    return value


def normalize(values, gain_vector):
    inv_scale = lax.rsqrt(jnp.mean(values * values, axis=-1, keepdims=True) + EPSILON)
    return values * inv_scale * gain_vector


def stats_block(hidden_rows, wanted, vocab_weight, voc_start):
    scores = jnp.dot(hidden_rows, vocab_weight, preferred_element_type=jnp.float32)
    highest = jnp.max(scores, axis=1)
    totals = jnp.sum(jnp.exp(scores - highest[:, None]), axis=1)
    columns = voc_start + lax.broadcasted_iota(jnp.int32, scores.shape, 1)
    picked = jnp.sum(jnp.where(columns == wanted[:, None], scores, 0.0), axis=1)
    return (highest, totals, picked)


def row_stats(hidden_rows, wanted, vocab_weight, voc_start):
    row_count = hidden_rows.shape[0]

    def one_block(packed):
        return stats_block(packed[0], packed[1], vocab_weight, voc_start)

    blocks = lax.map(
        one_block,
        (
            hidden_rows.reshape(row_count // 1024, 1024, hidden_rows.shape[1]),
            wanted.reshape(row_count // 1024, 1024),
        ),
    )
    return tuple((member.reshape(row_count) for member in blocks))


def join_rows(first, second):
    highest = jnp.maximum(first[0], second[0])
    totals = first[1] * jnp.exp(first[0] - highest) + second[1] * jnp.exp(second[0] - highest)
    return (highest, totals, first[2] + second[2])


def local(
    hidden_in,
    moe_gain,
    router_weight,
    expert_gate,
    expert_up,
    expert_down,
    final_gain,
    vocab_weight,
    token_ids,
    doc_ids,
    routes,
):
    tok_rows, width = hidden_in.shape
    owners = lax.axis_size(EXPERT)
    local_experts = expert_gate.shape[0]
    experts = owners * local_experts
    slot_count = max(2, 2 * TOP * tok_rows // experts)
    residual = hidden_in.astype(jnp.float32)
    normed = normalize(residual, moe_gain).astype(jnp.bfloat16)
    router_scores = jnp.dot(normed, router_weight, preferred_element_type=jnp.float32)
    chosen = routes[:, :, None] == lax.broadcasted_iota(jnp.int32, (tok_rows, TOP, experts), 2)
    picked_scores = jnp.sum(jnp.where(chosen, router_scores[:, None, :], 0.0), axis=2)
    first_gate = jax.nn.sigmoid(picked_scores[:, 0] - picked_scores[:, 1])
    second_gate = 1.0 - first_gate
    flat_routes = routes.reshape(tok_rows * TOP)
    one_hot = (
        flat_routes[:, None] == lax.broadcasted_iota(jnp.int32, (tok_rows * TOP, experts), 1)
    ).astype(jnp.int32)
    slot_index = jnp.sum(one_hot * jnp.cumsum(one_hot, axis=0), axis=1) - 1
    position = flat_routes * slot_count + slot_index
    slot_iota = lax.broadcasted_iota(jnp.int32, (tok_rows * TOP, experts * slot_count), 1)
    placement = (
        (position[:, None] == slot_iota)
        .astype(jnp.bfloat16)
        .reshape(tok_rows, TOP, experts * slot_count)
    )
    first_place = placement[:, 0, :]
    second_place = placement[:, 1, :]
    dispatch_map = first_place + second_place
    outgoing = lax.dot_general(
        dispatch_map, normed, (((0,), (0,)), ((), ())), preferred_element_type=jnp.float32
    )
    outgoing = outgoing.astype(jnp.bfloat16).reshape(owners, local_experts, slot_count, width)
    arrived = lax.all_to_all(outgoing, EXPERT, split_axis=0, concat_axis=0, tiled=True)
    gate_part = jnp.einsum(
        "sekd,edf->sekf", arrived, expert_gate, preferred_element_type=jnp.float32
    )
    up_part = jnp.einsum("sekd,edf->sekf", arrived, expert_up, preferred_element_type=jnp.float32)
    active = (jax.nn.silu(gate_part) * up_part).astype(jnp.bfloat16)
    expert_result = jnp.einsum(
        "sekf,efd->sekd", active, expert_down, preferred_element_type=jnp.float32
    ).astype(jnp.bfloat16)
    returned = lax.all_to_all(
        expert_result, EXPERT, split_axis=0, concat_axis=0, tiled=True
    ).reshape(experts * slot_count, width)
    first_rows = jnp.dot(first_place, returned, preferred_element_type=jnp.float32)
    second_rows = jnp.dot(second_place, returned, preferred_element_type=jnp.float32)
    mixed = residual + (first_gate[:, None] * first_rows + second_gate[:, None] * second_rows)
    final_rows = normalize(mixed, final_gain).astype(jnp.bfloat16)
    following = shifted((token_ids[:1], doc_ids[:1]), DP_EXPERT, -1)
    targets = jnp.concatenate([token_ids[1:], following[0]])
    counted = jnp.concatenate([doc_ids[1:], following[1]]) == doc_ids
    voc_start = lax.axis_index(EXPERT) * vocab_weight.shape[1]
    fresh = row_stats(
        lax.all_gather(final_rows, EXPERT, axis=0, tiled=True),
        lax.all_gather(targets, EXPERT, axis=0, tiled=True),
        vocab_weight,
        voc_start,
    )
    row_highest, row_totals, row_picked = tuple((update for update in fresh))
    own_start = lax.axis_index(EXPERT) * tok_rows
    merged = merged_by_axis((row_highest, row_totals, row_picked), EXPERT, join_rows)
    own_high = lax.dynamic_slice_in_dim(merged[0], own_start, tok_rows, 0)
    own_totals = lax.dynamic_slice_in_dim(merged[1], own_start, tok_rows, 0)
    target_score = lax.dynamic_slice_in_dim(merged[2], own_start, tok_rows, 0)
    log_norm = own_high + jnp.log(own_totals)
    token_loss = jnp.where(counted, log_norm - target_score, 0.0)
    devices = lax.axis_size("dp") * owners
    documents = DOC_DEV * devices
    doc_start = (lax.axis_index("dp") * owners + lax.axis_index(EXPERT)) * DOC_DEV
    member_map = (
        doc_ids[:, None] == lax.broadcasted_iota(jnp.int32, (tok_rows, documents), 1)
    ).astype(jnp.float32)
    partial_loss = jnp.dot(token_loss, member_map, precision=lax.Precision.HIGHEST)
    partial_length = jnp.sum(member_map, axis=0)
    whole_loss, whole_length = (
        by_axis(partial_loss, DP_EXPERT),
        by_axis(partial_length, DP_EXPERT),
    )
    loss_sum = jnp.sum(whole_loss)
    doc_loss = lax.dynamic_slice_in_dim(whole_loss, doc_start, DOC_DEV, 0)
    doc_length = lax.dynamic_slice_in_dim(whole_length, doc_start, DOC_DEV, 0)
    global_mean = loss_sum / (tok_rows * devices - documents)
    doc_score = doc_loss / doc_length - global_mean
    return (token_loss, doc_score)


def solution(mesh):
    split = Mesh(
        mesh.devices.reshape(mesh.shape["dp"], 4, 4, 2), ("dp", "expert_0", "expert_1", "expert_2")
    )
    in_specs = (
        P(DP_EXPERT, None),
        P(),
        P(),
        P(EXPERT, None, None),
        P(EXPERT, None, None),
        P(EXPERT, None, None),
        P(),
        P(None, EXPERT),
        P(DP_EXPERT),
        P(DP_EXPERT),
        P(DP_EXPERT, None),
    )
    out_specs = (P(DP_EXPERT), P(DP_EXPERT))
    return jax.shard_map(local, mesh=split, in_specs=in_specs, out_specs=out_specs, check_vma=False)
```

profile of v0, /device:TPU:1, one launch (start us, length us, event | category | flops | bytes accessed | tf_op | source)
XLA Modules:
  0.0 299.3 jit_solution(4102769667074141839)
XLA Ops:
  7.2 0.8 copy.47
  8.3 1.2 reduce-window.6
  10.2 0.7 multiply_add_fusion
  11.3 1.4 fusion.25
  12.7 1.9 convolution_convert_fusion
  14.7 37.4 %all_to_all.10 = bf16[32,2,16,1024]{3,2,1,0:T(8,128)(2,1)S(1)} all-to-all(bf16[32,2,16,1024]{3,2,1,0:T(8,128)(2,1)S(1)} %bitcast.274), channel_id=1, replica_groups=mesh['dp'=4,'expert_0'=4,'expert_1'=4,'expert_2'=2] {'expert_0','expert_..., dimensions={0} | all-to-all | bytes 4194304 | tf_op jit(solution)/shard_map/all_to_all | solution.py:134
  52.0 4.3 %fusion.8 = f32[2,32,16,1024]{3,2,1,0:T(8,128)} fusion(bf16[2,1024,1024]{2,1,0:T(8,128)(2,1)S(1)} %copy-done.7, bf16[32,2,16,1024]{3,2,1,0:T(8,128)(2,1)S(1)} %all_to_all.10), kind=kOutput, calls=%fused_computation.12 | convolution fusion | flops 2147483648 | bytes 10485760 | tf_op jit(solution)/shard_map/sekd,edf->sekf/dot_general | solution.py:135
  56.4 10.7 %convert_bitcast_fusion = bf16[32,2,16,1024]{3,2,0,1:T(8,128)(2,1)} fusion(bf16[2,1024,1024]{2,1,0:T(8,128)(2,1)} %param.18, f32[2,32,16,1024]{3,2,1,0:T(8,128)} %fusion.8, bf16[2,1024,1024]{2,1,0:T(8,128)(2,1)} %param.17, bf16[32,2,16,1024]{3,2,1,0:T(8,128)(2,1)S(1)} %all_to_all.10), kind=kOutput, calls=%fused_computation.21 | convolution fusion | flops 4302307328 | bytes 16777216 | tf_op jit(solution)/shard_map/sekf,efd->sekd/dot_general | solution.py:140
  67.0 3.3 %copy.53 = bf16[32,2,16,1024]{3,2,1,0:T(8,128)(2,1)} copy(bf16[32,2,16,1024]{3,2,0,1:T(8,128)(2,1)} %convert_bitcast_fusion) | data formatting | bytes 4194304 | tf_op jit(solution)/shard_map/convert_element_type | solution.py:142
  70.4 3.9 %all-to-all-start.1 = ((bf16[32,2,16,1024]{3,2,1,0:T(8,128)(2,1)}), bf16[32,2,16,1024]{3,2,1,0:T(8,128)(2,1)S(1)}, u32[]{:S(2)}, u32[]{:S(2)}) async-start(bf16[32,2,16,1024]{3,2,1,0:T(8,128)(2,1)} %copy.53), calls=%async_computation.1 | async-start | bytes 4194304 | tf_op jit(solution)/shard_map/all_to_all | solution.py:143
  74.8 27.8 %all-to-all-done.1 = bf16[32,2,16,1024]{3,2,1,0:T(8,128)(2,1)S(1)} async-done(((bf16[32,2,16,1024]{3,2,1,0:T(8,128)(2,1)}), bf16[32,2,16,1024]{3,2,1,0:T(8,128)(2,1)S(1)}, u32[]{:S(2)}, u32[]{:S(2)}) %all-to-all-start.1) | async-done | bytes 2097184 | tf_op jit(solution)/shard_map/all_to_all | solution.py:143
  102.6 0.7 convolution_multiply_fusion.1
  103.4 0.9 multiply_reduce_fusion
  104.4 1.0 multiply_convert_fusion
  105.3 0.6 slice.204
  105.9 2.8 collective-permute-start.1
  108.7 0.5 slice.194
  109.2 1.9 collective-permute-start
  111.4 0.7 pad_add_fusion
  112.1 24.1 %all-gather.3 = s32[32,1,256]{2,1,0:T(1,128)S(1)} all-gather(s32[1,1,256]{2,1,0:T(1,128)S(1)} %bitcast.293), channel_id=1, replica_groups=mesh['dp'=4,'expert_0'=4,'expert_1'=4,'expert_2'=2] {'expert_0','expert_..., dimensions={0}, use_global_device_ids=true | all-gather | bytes 33792 | tf_op jit(solution)/shard_map/all_gather | solution.py:156
  136.4 39.9 %all-gather.9.cloned.1.call-done = bf16[8192,1024]{1,0:T(8,128)(2,1)} async-done(((bf16[256,1024]{1,0:T(8,128)(2,1)}), bf16[8192,1024]{1,0:T(8,128)(2,1)}) %all-gather.9.cloned.1.call-update) | async-done | bytes 16777232 | tf_op jit(solution)/shard_map/all_gather | solution.py:155
  176.2 52.1 %while.14 = (s32[]{:T(128)}, f32[8,1024]{1,0:T(8,128)S(1)}, f32[8,1024]{1,0:T(8,128)S(1)}, f32[8,1024]{1,0:T(8,128)S(1)}, bf16[8,1024,1024]{2,1,0:T(8,128)(2,1)}...) while((s32[]{:T(128)}, f32[8,1024]{1,0:T(8,128)S(1)}, ...), condition=%wide.region_10.11_spmd, body=%wide.region_6.10_spmd.sunk | while | flops 2153773056 | bytes 12644985 | solution.py:74
  176.2 4.7 %fusion.87 = (f32[1024]{0:T(1024)S(1)}, f32[1024,1024]{0,1:T(8,128)S(1)}) fusion(bf16[1024,1024]{1,0:T(8,128)(2,1)} %get-tuple-element.175, bf16[8,1024,1024]{2,1,0:T(8,128)(2,1)} %get-tuple-element.174, s32[]{:T(128)} %get-tuple-element.160), kind=kOutput, calls=%fused_computation.133.clone.1 | convolution fusion | flops 2148531200 | bytes 8393216 | tf_op jit(solution)/shard_map/while/body/eval_jaxpr/dot_general | solution.py:60
  181.0 1.4 select_reduce_fusion.3
  182.8 4.7 %fusion.87 = (f32[1024]{0:T(1024)S(1)}, f32[1024,1024]{0,1:T(8,128)S(1)}) fusion(bf16[1024,1024]{1,0:T(8,128)(2,1)} %get-tuple-element.175, bf16[8,1024,1024]{2,1,0:T(8,128)(2,1)} %get-tuple-element.174, s32[]{:T(128)} %get-tuple-element.160), kind=kOutput, calls=%fused_computation.133.clone.1 | convolution fusion | flops 2148531200 | bytes 8393216 | tf_op jit(solution)/shard_map/while/body/eval_jaxpr/dot_general | solution.py:60
  187.5 1.4 select_reduce_fusion.3
  189.3 4.7 %fusion.87 = (f32[1024]{0:T(1024)S(1)}, f32[1024,1024]{0,1:T(8,128)S(1)}) fusion(bf16[1024,1024]{1,0:T(8,128)(2,1)} %get-tuple-element.175, bf16[8,1024,1024]{2,1,0:T(8,128)(2,1)} %get-tuple-element.174, s32[]{:T(128)} %get-tuple-element.160), kind=kOutput, calls=%fused_computation.133.clone.1 | convolution fusion | flops 2148531200 | bytes 8393216 | tf_op jit(solution)/shard_map/while/body/eval_jaxpr/dot_general | solution.py:60
  194.0 1.4 select_reduce_fusion.3
  195.8 4.7 %fusion.87 = (f32[1024]{0:T(1024)S(1)}, f32[1024,1024]{0,1:T(8,128)S(1)}) fusion(bf16[1024,1024]{1,0:T(8,128)(2,1)} %get-tuple-element.175, bf16[8,1024,1024]{2,1,0:T(8,128)(2,1)} %get-tuple-element.174, s32[]{:T(128)} %get-tuple-element.160), kind=kOutput, calls=%fused_computation.133.clone.1 | convolution fusion | flops 2148531200 | bytes 8393216 | tf_op jit(solution)/shard_map/while/body/eval_jaxpr/dot_general | solution.py:60
  200.5 1.4 select_reduce_fusion.3
  202.3 4.7 %fusion.87 = (f32[1024]{0:T(1024)S(1)}, f32[1024,1024]{0,1:T(8,128)S(1)}) fusion(bf16[1024,1024]{1,0:T(8,128)(2,1)} %get-tuple-element.175, bf16[8,1024,1024]{2,1,0:T(8,128)(2,1)} %get-tuple-element.174, s32[]{:T(128)} %get-tuple-element.160), kind=kOutput, calls=%fused_computation.133.clone.1 | convolution fusion | flops 2148531200 | bytes 8393216 | tf_op jit(solution)/shard_map/while/body/eval_jaxpr/dot_general | solution.py:60
  207.0 1.4 select_reduce_fusion.3
  208.8 4.7 %fusion.87 = (f32[1024]{0:T(1024)S(1)}, f32[1024,1024]{0,1:T(8,128)S(1)}) fusion(bf16[1024,1024]{1,0:T(8,128)(2,1)} %get-tuple-element.175, bf16[8,1024,1024]{2,1,0:T(8,128)(2,1)} %get-tuple-element.174, s32[]{:T(128)} %get-tuple-element.160), kind=kOutput, calls=%fused_computation.133.clone.1 | convolution fusion | flops 2148531200 | bytes 8393216 | tf_op jit(solution)/shard_map/while/body/eval_jaxpr/dot_general | solution.py:60
  213.5 1.4 select_reduce_fusion.3
  215.3 4.7 %fusion.87 = (f32[1024]{0:T(1024)S(1)}, f32[1024,1024]{0,1:T(8,128)S(1)}) fusion(bf16[1024,1024]{1,0:T(8,128)(2,1)} %get-tuple-element.175, bf16[8,1024,1024]{2,1,0:T(8,128)(2,1)} %get-tuple-element.174, s32[]{:T(128)} %get-tuple-element.160), kind=kOutput, calls=%fused_computation.133.clone.1 | convolution fusion | flops 2148531200 | bytes 8393216 | tf_op jit(solution)/shard_map/while/body/eval_jaxpr/dot_general | solution.py:60
  220.0 1.4 select_reduce_fusion.3
  221.8 4.7 %fusion.87 = (f32[1024]{0:T(1024)S(1)}, f32[1024,1024]{0,1:T(8,128)S(1)}) fusion(bf16[1024,1024]{1,0:T(8,128)(2,1)} %get-tuple-element.175, bf16[8,1024,1024]{2,1,0:T(8,128)(2,1)} %get-tuple-element.174, s32[]{:T(128)} %get-tuple-element.160), kind=kOutput, calls=%fused_computation.133.clone.1 | convolution fusion | flops 2148531200 | bytes 8393216 | tf_op jit(solution)/shard_map/while/body/eval_jaxpr/dot_general | solution.py:60
  226.5 1.4 select_reduce_fusion.3
  228.5 11.0 %all-gather.4 = f32[4,3,8192]{2,1,0:T(4,128)S(1)} all-gather(f32[1,3,8192]{2,1,0:T(4,128)S(1)} %maximum_bitcast_fusion), channel_id=2, replica_groups=mesh['dp'=4,'expert_0'=4,'expert_1'=4,'expert_2'=2] {'expert_0'}, dimensions={0}, use_global_device_ids=true | all-gather | bytes 491520 | tf_op jit(solution)/shard_map/all_gather | solution.py:30
  240.1 9.9 %all-gather.5 = f32[4,3,8192]{2,1,0:T(4,128)S(1)} all-gather(f32[1,3,8192]{2,1,0:T(4,128)S(1)} %maximum_bitcast_fusion.1), channel_id=3, replica_groups=mesh['dp'=4,'expert_0'=4,'expert_1'=4,'expert_2'=2] {'expert_1'}, dimensions={0}, use_global_device_ids=true | all-gather | bytes 491520 | tf_op jit(solution)/shard_map/all_gather | solution.py:30
  250.5 6.9 %all-gather.6 = f32[2,3,8192]{2,1,0:T(4,128)S(1)} all-gather(f32[1,3,8192]{2,1,0:T(4,128)S(1)} %maximum_bitcast_fusion.2), channel_id=4, replica_groups=mesh['dp'=4,'expert_0'=4,'expert_1'=4,'expert_2'=2] {'expert_2'}, dimensions={0}, use_global_device_ids=true | all-gather | bytes 294912 | tf_op jit(solution)/shard_map/all_gather | solution.py:30
  257.6 0.8 compare_select_fusion
  258.7 8.4 %all-reduce.2 = (f32[512]{0:T(512)S(1)}, f32[512]{0:T(512)S(1)}) all-reduce(f32[512]{0:T(512)S(1)} %convert_reduce_fusion, f32[512]{0:T(512)S(1)} %bitcast.294), channel_id=1, replica_groups=mesh['dp'=4,'expert_0'=4,'expert_1'=4,'expert_2'=2] {'dp'}, use_global_device_ids=true, to_apply=%region_16.17 | all-reduce | flops 1024 | bytes 8192 | tf_op jit(solution)/shard_map/psum | solution.py:50
  267.2 8.7 %all-reduce.1 = (f32[512]{0:T(512)S(1)}, f32[512]{0:T(512)S(1)}) all-reduce(f32[512]{0:T(512)S(1)} %get-tuple-element.71, f32[512]{0:T(512)S(1)} %get-tuple-element.72), channel_id=1, replica_groups=mesh['dp'=4,'expert_0'=4,'expert_1'=4,'expert_2'=2] {'expert_0'}, use_global_device_ids=true, to_apply=%region_17.18 | all-reduce | flops 1024 | bytes 8192 | tf_op jit(solution)/shard_map/psum | solution.py:50
  275.8 6.3 %all-reduce = (f32[512]{0:T(512)S(1)}, f32[512]{0:T(512)S(1)}) all-reduce(f32[512]{0:T(512)S(1)} %get-tuple-element.69, f32[512]{0:T(512)S(1)} %get-tuple-element.70), channel_id=1, replica_groups=mesh['dp'=4,'expert_0'=4,'expert_1'=4,'expert_2'=2] {'expert_1'}, use_global_device_ids=true, to_apply=%region_18.19 | all-reduce | flops 1024 | bytes 8192 | tf_op jit(solution)/shard_map/psum | solution.py:50
  282.1 8.5 %all-reduce.3 = (f32[512]{0:T(512)S(1)}, f32[512]{0:T(512)S(1)}) all-reduce(f32[512]{0:T(512)S(1)} %get-tuple-element.67, f32[512]{0:T(512)S(1)} %get-tuple-element.68), channel_id=1, replica_groups=mesh['dp'=4,'expert_0'=4,'expert_1'=4,'expert_2'=2] {'expert_2'}, use_global_device_ids=true, to_apply=%region_19.20 | all-reduce | flops 1024 | bytes 8192 | tf_op jit(solution)/shard_map/psum | solution.py:50
  290.6 0.6 reduce_sum.77
  291.9 0.6 fusion.73
  (100 shorter events, 6.7 us)
Async XLA Ops:
  7.2 67.2 %copy-start = (bf16[1024,64]{0,1:T(8,128)(2,1)S(1)}, bf16[1024,64]{0,1:T(8,128)(2,1)}, u32[]{:S(2)}) copy-start(bf16[1024,64]{0,1:T(8,128)(2,1)} %param.15) | copy-start | bytes 393220
  11.3 40.7 %copy-start.7 = (bf16[2,1024,1024]{2,1,0:T(8,128)(2,1)S(1)}, bf16[2,1024,1024]{2,1,0:T(8,128)(2,1)}, u32[]{:S(2)}) copy-start(bf16[2,1024,1024]{2,1,0:T(8,128)(2,1)} %param.16) | copy-start | bytes 12582916
  67.0 7.3 %copy-start.1 = (bf16[256,1024]{1,0:T(8,128)(2,1)S(1)}, bf16[256,1024]{1,0:T(8,128)(2,1)}, u32[]{:S(2)}) copy-start(bf16[256,1024]{1,0:T(8,128)(2,1)} %param.13) | copy-start | bytes 1572868
  67.0 7.3 %copy-start.8 = (f32[1024]{0:T(1024)S(1)}, f32[1024]{0:T(1024)}, u32[]{:S(2)}) copy-start(f32[1024]{0:T(1024)} %param.14) | copy-start | bytes 12292
  67.0 7.7 %copy-start.2 = (s32[256,2]{0,1:T(2,128)S(1)}, s32[256,2]{0,1:T(2,128)}, u32[]{:S(2)}) copy-start(s32[256,2]{0,1:T(2,128)} %param.23) | copy-start | bytes 6148
  70.4 32.3 %all-to-all-start.1 = ((bf16[32,2,16,1024]{3,2,1,0:T(8,128)(2,1)}), bf16[32,2,16,1024]{3,2,1,0:T(8,128)(2,1)S(1)}, u32[]{:S(2)}, u32[]{:S(2)}) async-start(bf16[32,2,16,1024]{3,2,1,0:T(8,128)(2,1)} %copy.53), calls=%async_computation.1 | async-start | bytes 4194304 | tf_op jit(solution)/shard_map/all_to_all | solution.py:143
  74.3 101.9 %all-gather.9.cloned.1.call-start = ((), (), s32[]{:S(2)}) async-start(), calls=%async_computation.2 | async-start | bytes 17301504 | tf_op jit(solution)/shard_map/all_gather | solution.py:155
  102.6 1.7 copy-start.4
  103.4 2.0 copy-start.6
  103.4 5.3 %copy-start.3 = (s32[256]{0:T(256)S(1)}, s32[256]{0:T(256)}, u32[]{:S(2)}) copy-start(s32[256]{0:T(256)} %param.22) | copy-start | bytes 3076
  105.9 5.5 %collective-permute-start.1 = (s32[1]{0:T(128)}, s32[1]{0:T(128)}, u32[]{:S(2)}, u32[]{:S(2)}) collective-permute-start(s32[1]{0:T(128)} %slice.204), channel_id=1, source_target_pairs={{1,0},{2,1},{3,2},{4,3},{5,4},{6,5},{7,6},{8,7},{9,8},{10,9},{11,1... | collective-permute-start | bytes 20 | tf_op jit(solution)/shard_map/ppermute | solution.py:19
  109.2 148.4 %collective-permute-start = (s32[1]{0:T(128)}, s32[1]{0:T(128)}, u32[]{:S(2)}, u32[]{:S(2)}) collective-permute-start(s32[1]{0:T(128)} %slice.194), channel_id=1, source_target_pairs={{1,0},{2,1},{3,2},{4,3},{5,4},{6,5},{7,6},{8,7},{9,8},{10,9},{11,1... | collective-permute-start | bytes 20 | tf_op jit(solution)/shard_map/ppermute | solution.py:19
  258.4 34.1 %copy-start.5 = (f32[256]{0:T(256)}, f32[256]{0:T(256)S(1)}, u32[]{:S(2)}) copy-start(f32[256]{0:T(256)S(1)} %compare_select_fusion) | copy-start | bytes 3076
Sparse Core Ops, SparseCore 0:
  105.5 70.7 all-gather.8
where the time goes:
time: 300 us; the launch traced here: 299 us
  blocking collectives  121 us (40%)
  waiting for transfers between devices  67.7 us (23%)
  matrix products  56.8 us (19%)
  other arithmetic  20.3 us (7%)
  between operations  15 us (5%)
  local copies, waits for them, and re-layouts  9.12 us (3%)
  starting transfers between devices  8.66 us (3%)
    all_gather x1, waiting for transfers between devices, local(): lax.all_gather(final_rows, EXPERT, axis=0, tiled=True)  39.9 us
    dot_general x8, matrix products, stats_block(): jnp.dot(hidden_rows, vocab_weight, preferred_element_type=jnp.float32)  37.5 us
    all_to_all x1, blocking collectives, local(): lax.all_to_all(outgoing, EXPERT, split_axis=0, concat_axis=0, tiled=True)  37.4 us
    psum x4, blocking collectives, by_axis(): value = lax.psum(value, axis)  31.9 us
    all_to_all x1, waiting for transfers between devices, local(): lax.all_to_all(expert_result, EXPERT, split_axis=0, concat_axis=0, tiled=...  27.8 us
    all_gather x3, blocking collectives, gathered_once(): both, at, found = (lax.all_gather(jnp.concatenate(lines), axis), 0, {})  27.8 us
    all_gather x1, blocking collectives, local(): lax.all_gather(targets, EXPERT, axis=0, tiled=True)  24.1 us
    reduce_sum x8, other arithmetic, stats_block(): picked = jnp.sum(jnp.where(columns == wanted[:, None], scores, 0.0), axis=1)  11.3 us
  transfers between devices with their start and end apart: 4, of which 2 were waited for; matrix products, arithmetic and copies ran while one was open for 19% of the time, Pallas kernels for 0%

commit v1 on v0

v1 whole, which is shorter than its diff:
```python
import jax
import jax.numpy as jnp
from jax import lax
from jax.experimental import pallas as pl
from jax.experimental.pallas import tpu as pltpu
from jax.sharding import PartitionSpec as P

TOP = 2
DOC_DEV = 4
SIDE = 4
OWNERS = 32
GROUPS = 4
BOTH = ("dp", "expert")
EPSILON = 1e-06
MESH_ID = pl.DeviceIdType.MESH


def normalize(values, gain_vector):
    inv_scale = lax.rsqrt(jnp.mean(values * values, axis=-1, keepdims=True) + EPSILON)
    return values * inv_scale * gain_vector


def place():
    own = lax.axis_index("expert")
    return own // 8, (own // 2) % SIDE, own % 2


def partner(i, sign):
    x, z, core = place()
    dx = (i % 8) // 2
    dz = (i // 8 + SIDE - dx) % SIDE
    dc = i % 2
    return ((x + sign * dx + SIDE) % SIDE) * 8 + ((z + sign * dz + SIDE) % SIDE) * 2 + (core + dc) % 2


def moe_kernel(
    hidden_ref, gain_ref, router_ref, routes_ref, final_gain_ref, gate_hbm, up_hbm, down_hbm,
    rows_ref,
    normed, outgoing, arrived, gate_w, up_w, down_w, result, returned, place_a, place_b, mixed,
    weight_sem, self_sem, send_out, recv_out, send_back, recv_back,
):
    tokens, width = hidden_ref.shape
    local = gate_hbm.shape[0]
    experts = OWNERS * local
    slots = outgoing.shape[2]
    part = local * slots
    per_group = OWNERS // GROUPS
    chunk = per_group * slots
    barrier = pltpu.get_barrier_semaphore()
    dp = lax.axis_index("dp")

    def to(device):
        return {"dp": dp, "expert": device}

    @pl.loop(1, OWNERS)
    def _(i):
        pl.semaphore_signal(barrier, inc=1, device_id=to(partner(i, 1)), device_id_type=MESH_ID)

    weights = []
    for n, (source, target) in enumerate(((gate_hbm, gate_w), (up_hbm, up_w), (down_hbm, down_w))):
        copy = pltpu.make_async_copy(source, target, weight_sem.at[n])
        copy.start()
        weights.append(copy)

    residual = hidden_ref[...].astype(jnp.float32)
    normed[...] = normalize(residual, gain_ref[...]).astype(jnp.bfloat16)
    router_scores = lax.dot_general(
        router_ref[...], normed[...], (((1,), (1,)), ((), ())), preferred_element_type=jnp.float32
    )
    first = routes_ref[0:1, :]
    second = routes_ref[1:2, :]
    expert_iota = lax.broadcasted_iota(jnp.int32, (experts, tokens), 0)
    is_first = expert_iota == first
    is_second = expert_iota == second
    member = jnp.where(is_first | is_second, 1.0, 0.0).astype(jnp.bfloat16)
    earlier = (
        lax.broadcasted_iota(jnp.int32, (tokens, tokens), 0) < lax.broadcasted_iota(jnp.int32, (tokens, tokens), 1)
    )
    rank = jnp.dot(
        member, jnp.where(earlier, 1.0, 0.0).astype(jnp.bfloat16), preferred_element_type=jnp.float32
    )
    x, z, core = place()

    def position(expert, chosen):
        owner = expert // local
        dx = (owner // 8 + SIDE - x) % SIDE
        dz = ((owner // 2) % SIDE + SIDE - z) % SIDE
        dc = (owner + core) % 2
        index = ((dx + dz) % SIDE) * 8 + dx * 2 + dc
        own_rank = jnp.sum(jnp.where(chosen, rank, 0.0), axis=0, keepdims=True).astype(jnp.int32)
        return index * part + (expert % local) * slots + own_rank

    first_pos = position(first, is_first)
    second_pos = position(second, is_second)

    for group in range(GROUPS):
        slot_iota = lax.broadcasted_iota(jnp.int32, (per_group * part, tokens), 0) + group * per_group * part
        chosen = (slot_iota == first_pos) | (slot_iota == second_pos)
        block = jnp.dot(
            jnp.where(chosen, 1.0, 0.0).astype(jnp.bfloat16), normed[...], preferred_element_type=jnp.float32
        )
        outgoing[pl.ds(group * per_group, per_group)] = block.astype(jnp.bfloat16).reshape(
            per_group, local, slots, width
        )
        if group == 0:
            own_copy = pltpu.make_async_copy(outgoing.at[0], arrived.at[:, pl.ds(0, slots)], self_sem)
            own_copy.start()
            pl.semaphore_wait(barrier, OWNERS - 1)

        @pl.loop(max(1, group * per_group), (group + 1) * per_group)
        def _(i):
            pltpu.make_async_remote_copy(
                src_ref=outgoing.at[i],
                dst_ref=arrived.at[:, pl.ds(pl.multiple_of(i * slots, slots), slots)],
                send_sem=send_out.at[i],
                recv_sem=recv_out.at[i],
                device_id=to(partner(i, 1)),
                device_id_type=MESH_ID,
            ).start()

    picked = jnp.sum(
        jnp.where(is_first, router_scores, 0.0) - jnp.where(is_second, router_scores, 0.0), axis=0, keepdims=True
    )
    first_gate = jax.nn.sigmoid(picked)
    lines = lax.broadcasted_iota(jnp.int32, (128, tokens), 0)
    table = jnp.where(
        lines == 0,
        first_pos.astype(jnp.float32),
        jnp.where(lines == 1, second_pos.astype(jnp.float32), jnp.where(lines == 2, first_gate, 0.0)),
    )
    columns = table.T
    lane_iota = lax.broadcasted_iota(jnp.int32, (tokens, experts * slots), 1).astype(jnp.float32)
    place_a[...] = jnp.where(lane_iota == columns[:, 0:1], 1.0, 0.0).astype(jnp.bfloat16)
    place_b[...] = jnp.where(lane_iota == columns[:, 1:2], 1.0, 0.0).astype(jnp.bfloat16)
    gate_a = columns[:, 2:3]
    gate_b = 1.0 - gate_a

    own_copy.wait()
    for copy in weights:
        copy.wait()

    def arrival(i):
        return pltpu.make_async_remote_copy(
            src_ref=outgoing.at[i],
            dst_ref=arrived.at[:, pl.ds(pl.multiple_of(i * slots, slots), slots)],
            send_sem=send_out.at[i],
            recv_sem=recv_out.at[i],
            device_id=to(partner(i, 1)),
            device_id_type=MESH_ID,
        )

    def back(i):
        return pltpu.make_async_remote_copy(
            src_ref=result.at[:, pl.ds(pl.multiple_of(i * slots, slots), slots)],
            dst_ref=returned.at[i],
            send_sem=send_back.at[i],
            recv_sem=recv_back.at[i],
            device_id=to(partner(i, -1)),
            device_id_type=MESH_ID,
        )

    for group in range(GROUPS):
        low, high = max(1, group * per_group), (group + 1) * per_group

        @pl.loop(low, high)
        def _(i):
            arrival(i).wait_recv()

        @pl.loop(0, local)
        def _(n):
            inputs = arrived[n, pl.ds(group * chunk, chunk)]
            gate_part = jnp.dot(inputs, gate_w[n], preferred_element_type=jnp.float32)
            up_part = jnp.dot(inputs, up_w[n], preferred_element_type=jnp.float32)
            active = (jax.nn.silu(gate_part) * up_part).astype(jnp.bfloat16)
            result[n, pl.ds(group * chunk, chunk)] = jnp.dot(
                active, down_w[n], preferred_element_type=jnp.float32
            ).astype(jnp.bfloat16)

        if group == 0:
            home = pltpu.make_async_copy(result.at[:, pl.ds(0, slots)], returned.at[0], self_sem)
            home.start()

        @pl.loop(low, high)
        def _(i):
            back(i).start()

    home.wait()
    mixed[...] = residual
    for group in range(GROUPS):
        low, high = max(1, group * per_group), (group + 1) * per_group

        @pl.loop(low, high)
        def _(i):
            back(i).wait_recv()

        block = returned[pl.ds(group * per_group, per_group)].reshape(per_group * part, width)
        span = slice(group * per_group * part, (group + 1) * per_group * part)
        mixed[...] += gate_a * jnp.dot(
            place_a[:, span], block, preferred_element_type=jnp.float32
        ) + gate_b * jnp.dot(place_b[:, span], block, preferred_element_type=jnp.float32)
    rows_ref[...] = normalize(mixed[...], final_gain_ref[...]).astype(jnp.bfloat16)

    @pl.loop(1, OWNERS)
    def _(i):
        arrival(i).wait_send()
        back(i).wait_send()


def moe(hidden_in, moe_gain, router_weight, expert_gate, expert_up, expert_down, final_gain, routes):
    tokens, width = hidden_in.shape
    local, _, hidden_units = expert_gate.shape
    experts = OWNERS * local
    slots = max(2, 2 * TOP * tokens // experts)
    bf16, f32 = jnp.bfloat16, jnp.float32
    vmem = pl.BlockSpec(memory_space=pltpu.VMEM)
    hbm = pl.BlockSpec(memory_space=pl.ANY)
    return pl.pallas_call(
        moe_kernel,
        out_shape=jax.ShapeDtypeStruct((tokens, width), bf16),
        in_specs=[vmem] * 5 + [hbm] * 3,
        out_specs=vmem,
        scratch_shapes=[
            pltpu.VMEM((tokens, width), bf16),
            pltpu.VMEM((OWNERS, local, slots, width), bf16),
            pltpu.VMEM((local, OWNERS * slots, width), bf16),
            pltpu.VMEM((local, width, hidden_units), bf16),
            pltpu.VMEM((local, width, hidden_units), bf16),
            pltpu.VMEM((local, hidden_units, width), bf16),
            pltpu.VMEM((local, OWNERS * slots, width), bf16),
            pltpu.VMEM((OWNERS, local, slots, width), bf16),
            pltpu.VMEM((tokens, experts * slots), bf16),
            pltpu.VMEM((tokens, experts * slots), bf16),
            pltpu.VMEM((tokens, width), f32),
            pltpu.SemaphoreType.DMA((3,)),
            pltpu.SemaphoreType.DMA,
            pltpu.SemaphoreType.DMA((OWNERS,)),
            pltpu.SemaphoreType.DMA((OWNERS,)),
            pltpu.SemaphoreType.DMA((OWNERS,)),
            pltpu.SemaphoreType.DMA((OWNERS,)),
        ],
        compiler_params=pltpu.CompilerParams(
            collective_id=0, has_side_effects=True, vmem_limit_bytes=48 * 2**20
        ),
        name="moe",
    )(
        hidden_in, moe_gain.reshape(1, width), router_weight.T, routes.T, final_gain.reshape(1, width),
        expert_gate, expert_up, expert_down,
    )


def stats_block(hidden_rows, wanted, vocab_weight, voc_start):
    scores = jnp.dot(hidden_rows, vocab_weight, preferred_element_type=jnp.float32)
    highest = jnp.max(scores, axis=1)
    totals = jnp.sum(jnp.exp(scores - highest[:, None]), axis=1)
    columns = voc_start + lax.broadcasted_iota(jnp.int32, scores.shape, 1)
    picked = jnp.sum(jnp.where(columns == wanted[:, None], scores, 0.0), axis=1)
    return jnp.stack([highest, totals, picked])


def local(
    hidden_in, moe_gain, router_weight, expert_gate, expert_up, expert_down, final_gain, vocab_weight,
    token_ids, doc_ids, routes,
):
    tok_rows, width = hidden_in.shape
    devices = lax.axis_size("dp") * OWNERS
    final_rows = moe(hidden_in, moe_gain, router_weight, expert_gate, expert_up, expert_down, final_gain, routes)
    heads = jnp.stack([token_ids[0], doc_ids[0]])
    following = lax.ppermute(heads, BOTH, [(k + 1, k) for k in range(devices - 1)])
    targets = jnp.concatenate([token_ids[1:], following[:1]])
    own = lax.axis_index("dp") * OWNERS + lax.axis_index("expert")
    doc_next = jnp.where(own == devices - 1, -1, following[1:])
    counted = jnp.concatenate([doc_ids[1:], doc_next]) == doc_ids
    voc_start = lax.axis_index("expert") * vocab_weight.shape[1]
    all_rows = lax.all_gather(final_rows, "expert", axis=0, tiled=True)
    all_targets = lax.all_gather(targets, "expert", axis=0, tiled=True)
    blocks = lax.map(
        lambda packed: stats_block(packed[0], packed[1], vocab_weight, voc_start),
        (all_rows.reshape(8, 1024, width), all_targets.reshape(8, 1024)),
    )
    stats = jnp.transpose(blocks, (0, 2, 1)).reshape(OWNERS, tok_rows, 3)
    stats = jnp.transpose(stats, (0, 2, 1))
    mine = lax.all_to_all(stats, "expert", split_axis=0, concat_axis=0, tiled=True)
    high = jnp.max(mine[:, 0], axis=0)
    totals = jnp.sum(mine[:, 1] * jnp.exp(mine[:, 0] - high), axis=0)
    token_loss = jnp.where(counted, high + jnp.log(totals) - jnp.sum(mine[:, 2], axis=0), 0.0)
    documents = DOC_DEV * devices
    member_map = (doc_ids[:, None] == lax.broadcasted_iota(jnp.int32, (tok_rows, documents), 1)).astype(jnp.float32)
    partial = jnp.stack(
        [jnp.dot(token_loss, member_map, precision=lax.Precision.HIGHEST), jnp.sum(member_map, axis=0)]
    )
    whole = lax.psum(partial, BOTH)
    pieces = lax.dynamic_slice_in_dim(whole, own * DOC_DEV, DOC_DEV, 1)
    global_mean = jnp.sum(whole[0]) / (tok_rows * devices - documents)
    return (token_loss, pieces[0] / pieces[1] - global_mean)


def solution(mesh):
    in_specs = (
        P(BOTH, None), P(), P(), P("expert", None, None), P("expert", None, None), P("expert", None, None), P(),
        P(None, "expert"), P(BOTH), P(BOTH), P(BOTH, None),
    )
    return jax.shard_map(local, mesh=mesh, in_specs=in_specs, out_specs=(P(BOTH), P(BOTH)), check_vma=False)
```

time: 300 us -> 285 us (0.950)
  Pallas kernels: 0 us -> 65.5 us
  blocking collectives: 121 us -> 89.1 us
  matrix products: 56.8 us -> 33.1 us
  waiting for transfers between devices: 67.7 us -> 48.7 us
  other arithmetic: 20.3 us -> 15.2 us
    pallas_call x0 -> x1, Pallas kernels: none -> 65.5 us  [moe(): pl.pallas_call(moe_kernel, out_shape=jax.ShapeDtypeStruct((tokens, width)...]
    all_to_all x1 -> x0, blocking collectives: 37.4 us -> none  [local(): lax.all_to_all(outgoing, EXPERT, split_axis=0, concat_axis=0, tiled=True)]
    psum x4 -> x1, blocking collectives: 31.9 us -> 64.2 us  [local(): whole = lax.psum(partial, BOTH)]
    all_gather x4 -> x1, blocking collectives: 51.9 us -> 24.9 us  [local(): all_targets = lax.all_gather(targets, 'expert', axis=0, tiled=True)]
    all_to_all x1, waiting for transfers between devices: 27.8 us -> 7 us  [local(): lax.all_to_all(stats, 'expert', split_axis=0, concat_axis=0, tiled=True)]
    dot_general x6 -> x0, matrix products: 18.9 us -> none  [the longest x1 10.7 us: local(): jnp.einsum('sekf,efd->sekd', active, expert_down, preferred_element_type=...]
    unnamed x22 -> x20, local copies, waits for them, and re-layouts: 1 us -> 6.19 us
    dot_general x8, matrix products: 37.5 us -> 32.8 us  [stats_block(): jnp.dot(hidden_rows, vocab_weight, preferred_element_type=jnp.float32)]
  transfers between devices with their start and end apart: 4 -> 3, of which waited for: 2 -> 3; matrix products, arithmetic and copies ran while one was open for 19% -> 1% of each run, Pallas kernels for 0% -> 0%
where the time goes in v1:
time: 285 us; the launch traced here: 284 us
  blocking collectives  89.1 us (31%)
  Pallas kernels  65.5 us (23%)
  waiting for transfers between devices  48.7 us (17%)
  matrix products  33.1 us (12%)
  between operations  15.4 us (5%)
  other arithmetic  15.2 us (5%)
  local copies, waits for them, and re-layouts  8.91 us (3%)
  starting transfers between devices  8.17 us (3%)
    pallas_call x1, Pallas kernels, moe(): pl.pallas_call(moe_kernel, out_shape=jax.ShapeDtypeStruct((tokens, width)...  65.5 us
    psum x1, blocking collectives, local(): whole = lax.psum(partial, BOTH)  64.2 us
    all_gather x1, waiting for transfers between devices, local(): all_rows = lax.all_gather(final_rows, 'expert', axis=0, tiled=True)  39.8 us
    dot_general x8, matrix products, stats_block(): jnp.dot(hidden_rows, vocab_weight, preferred_element_type=jnp.float32)  32.8 us
    all_gather x1, blocking collectives, local(): all_targets = lax.all_gather(targets, 'expert', axis=0, tiled=True)  24.9 us
    reduce_sum x8, other arithmetic, stats_block(): totals = jnp.sum(jnp.exp(scores - highest[:, None]), axis=1)  11.3 us
    all_to_all x1, waiting for transfers between devices, local(): lax.all_to_all(stats, 'expert', split_axis=0, concat_axis=0, tiled=True)  7 us
    unnamed x20, local copies, waits for them, and re-layouts  6.19 us
  transfers between devices with their start and end apart: 3, of which 3 were waited for; matrix products, arithmetic and copies ran while one was open for 1% of the time, Pallas kernels for 0%

profile of v1, /device:TPU:1, one launch (start us, length us, event | category | flops | bytes accessed | tf_op | source)
XLA Modules:
  0.0 284.4 jit_solution(1950725445365030520)
XLA Ops:
  7.2 2.2 copy-done
  9.4 1.0 copy-done.1
  10.4 0.9 copy-done.2
  11.4 0.7 copy-done.3
  12.0 0.7 copy-done.4
  12.7 0.7 copy-done.5
  13.4 65.5 %moe.1 = bf16[256,1024]{1,0:T(8,128)(2,1)} custom-call(bf16[256,1024]{1,0:T(8,128)(2,1)S(1)} %copy-done.1, f32[1,1024]{1,0:T(1,128)S(1)} %bitcast.60, bf16[64,1024]{1,0:T(8,128)(2,1)S(1)} %bitcast.59, s32[2,256]{1,0:T(2,128)S(1)} %bitcast.62, f32[1,1024]{1,0:T(1,128)S(1)} %bitcast.61, bf16[2,1024,1024]{2,1,0:T(8,128)(2,1)S(1)} %copy-done, ...), custom_call_target="tpu_custom_call" | custom-call | tf_op jit(solution)/shard_map/moe/pallas_call | solution.py:217
  78.9 0.5 slice.38
  79.5 0.5 slice.39
  80.0 1.4 pad_add_fusion.1
  81.3 2.7 collective-permute-start
  84.1 0.1 slice.41
  84.2 0.1 slice.37
  84.2 1.9 collective-permute-done
  86.2 0.6 fusion.12
  86.7 0.7 pad_add_fusion
  87.5 24.9 %all-gather = s32[32,1,256]{2,1,0:T(1,128)S(1)} all-gather(s32[1,1,256]{2,1,0:T(1,128)S(1)} %bitcast.70), channel_id=1, replica_groups=mesh['dp'=4,'expert'=32] {'expert'}, dimensions={0}, use_global_device_ids=true | all-gather | bytes 33792 | tf_op jit(solution)/shard_map/all_gather | solution.py:275
  112.4 0.1 reduce.3
  112.5 39.8 %all-gather.3.cloned.1.call-done = bf16[8192,1024]{1,0:T(8,128)(2,1)} async-done(((bf16[256,1024]{1,0:T(8,128)(2,1)}), bf16[8192,1024]{1,0:T(8,128)(2,1)}) %all-gather.3.cloned.1.call-update) | async-done | bytes 16777232 | tf_op jit(solution)/shard_map/all_gather | solution.py:274
  152.3 44.8 %while.10 = (s32[]{:T(128)}, f32[8,3,1024]{2,1,0:T(4,128)S(1)}, bf16[8,1024,1024]{2,1,0:T(8,128)(2,1)}, bf16[1024,1024]{1,0:T(8,128)(2,1)S(1)}, s32[]{:T(128)}, /*index=5*/s32[8,1024]{1,0:T(8,128)S(1)}, s32[]{:T(128)}) while((s32[]{:T(128)}, f32[8,3,1024]{2,1,0:T(4,128)S(1)}, bf16[8,1024,1024]{2,1,0:T(8,128)(2,1)}, ...), condition=%wide.region_4.5_spmd, body=%wide.region_0.4_spmd.sunk | while | flops 2153779200 | bytes 12649049 | solution.py:276
  152.3 4.1 %fusion.19 = (f32[1024]{0:T(1024)S(1)}, f32[1024,1024]{0,1:T(8,128)S(1)}) fusion(bf16[1024,1024]{1,0:T(8,128)(2,1)S(1)} %get-tuple-element.119, bf16[8,1024,1024]{2,1,0:T(8,128)(2,1)} %get-tuple-element.118, s32[]{:T(128)} %get-tuple-element.109), kind=kOutput, calls=%fused_computation.30.clone.1 | convolution fusion | flops 2148531200 | bytes 8393216 | tf_op jit(solution)/shard_map/while/body/eval_jaxpr/dot_general | solution.py:252
  156.4 1.4 exponential_reduce_fusion.2
  157.8 4.1 %fusion.19 = (f32[1024]{0:T(1024)S(1)}, f32[1024,1024]{0,1:T(8,128)S(1)}) fusion(bf16[1024,1024]{1,0:T(8,128)(2,1)S(1)} %get-tuple-element.119, bf16[8,1024,1024]{2,1,0:T(8,128)(2,1)} %get-tuple-element.118, s32[]{:T(128)} %get-tuple-element.109), kind=kOutput, calls=%fused_computation.30.clone.1 | convolution fusion | flops 2148531200 | bytes 8393216 | tf_op jit(solution)/shard_map/while/body/eval_jaxpr/dot_general | solution.py:252
  162.0 1.4 exponential_reduce_fusion.2
  163.4 4.1 %fusion.19 = (f32[1024]{0:T(1024)S(1)}, f32[1024,1024]{0,1:T(8,128)S(1)}) fusion(bf16[1024,1024]{1,0:T(8,128)(2,1)S(1)} %get-tuple-element.119, bf16[8,1024,1024]{2,1,0:T(8,128)(2,1)} %get-tuple-element.118, s32[]{:T(128)} %get-tuple-element.109), kind=kOutput, calls=%fused_computation.30.clone.1 | convolution fusion | flops 2148531200 | bytes 8393216 | tf_op jit(solution)/shard_map/while/body/eval_jaxpr/dot_general | solution.py:252
  167.6 1.4 exponential_reduce_fusion.2
  169.0 4.1 %fusion.19 = (f32[1024]{0:T(1024)S(1)}, f32[1024,1024]{0,1:T(8,128)S(1)}) fusion(bf16[1024,1024]{1,0:T(8,128)(2,1)S(1)} %get-tuple-element.119, bf16[8,1024,1024]{2,1,0:T(8,128)(2,1)} %get-tuple-element.118, s32[]{:T(128)} %get-tuple-element.109), kind=kOutput, calls=%fused_computation.30.clone.1 | convolution fusion | flops 2148531200 | bytes 8393216 | tf_op jit(solution)/shard_map/while/body/eval_jaxpr/dot_general | solution.py:252
  173.2 1.4 exponential_reduce_fusion.2
  174.6 4.1 %fusion.19 = (f32[1024]{0:T(1024)S(1)}, f32[1024,1024]{0,1:T(8,128)S(1)}) fusion(bf16[1024,1024]{1,0:T(8,128)(2,1)S(1)} %get-tuple-element.119, bf16[8,1024,1024]{2,1,0:T(8,128)(2,1)} %get-tuple-element.118, s32[]{:T(128)} %get-tuple-element.109), kind=kOutput, calls=%fused_computation.30.clone.1 | convolution fusion | flops 2148531200 | bytes 8393216 | tf_op jit(solution)/shard_map/while/body/eval_jaxpr/dot_general | solution.py:252
  178.8 1.4 exponential_reduce_fusion.2
  180.2 4.1 %fusion.19 = (f32[1024]{0:T(1024)S(1)}, f32[1024,1024]{0,1:T(8,128)S(1)}) fusion(bf16[1024,1024]{1,0:T(8,128)(2,1)S(1)} %get-tuple-element.119, bf16[8,1024,1024]{2,1,0:T(8,128)(2,1)} %get-tuple-element.118, s32[]{:T(128)} %get-tuple-element.109), kind=kOutput, calls=%fused_computation.30.clone.1 | convolution fusion | flops 2148531200 | bytes 8393216 | tf_op jit(solution)/shard_map/while/body/eval_jaxpr/dot_general | solution.py:252
  184.4 1.4 exponential_reduce_fusion.2
  185.8 4.1 %fusion.19 = (f32[1024]{0:T(1024)S(1)}, f32[1024,1024]{0,1:T(8,128)S(1)}) fusion(bf16[1024,1024]{1,0:T(8,128)(2,1)S(1)} %get-tuple-element.119, bf16[8,1024,1024]{2,1,0:T(8,128)(2,1)} %get-tuple-element.118, s32[]{:T(128)} %get-tuple-element.109), kind=kOutput, calls=%fused_computation.30.clone.1 | convolution fusion | flops 2148531200 | bytes 8393216 | tf_op jit(solution)/shard_map/while/body/eval_jaxpr/dot_general | solution.py:252
  190.0 1.4 exponential_reduce_fusion.2
  191.4 4.1 %fusion.19 = (f32[1024]{0:T(1024)S(1)}, f32[1024,1024]{0,1:T(8,128)S(1)}) fusion(bf16[1024,1024]{1,0:T(8,128)(2,1)S(1)} %get-tuple-element.119, bf16[8,1024,1024]{2,1,0:T(8,128)(2,1)} %get-tuple-element.118, s32[]{:T(128)} %get-tuple-element.109), kind=kOutput, calls=%fused_computation.30.clone.1 | convolution fusion | flops 2148531200 | bytes 8393216 | tf_op jit(solution)/shard_map/while/body/eval_jaxpr/dot_general | solution.py:252
  195.6 1.4 exponential_reduce_fusion.2
  197.0 0.1 copy.19
  197.1 0.7 copy.20
  197.8 5.4 %all-to-all-start = ((f32[32,3,256]{2,1,0:T(4,128)}), f32[32,3,256]{2,1,0:T(4,128)S(1)}, u32[]{:S(2)}, u32[]{:S(2)}) async-start(f32[32,3,256]{2,1,0:T(4,128)} %copy.20), calls=%async_computation | async-start | bytes 262144 | tf_op jit(solution)/shard_map/all_to_all | solution.py:282
  203.2 0.1 convert_reduce_fusion
  203.9 7.0 %all-to-all-done = f32[32,3,256]{2,1,0:T(4,128)S(1)} async-done(((f32[32,3,256]{2,1,0:T(4,128)}), f32[32,3,256]{2,1,0:T(4,128)S(1)}, u32[]{:S(2)}, u32[]{:S(2)}) %all-to-all-start) | async-done | bytes 98336 | tf_op jit(solution)/shard_map/all_to_all | solution.py:282
  210.9 0.1 slice_reduce_fusion.2
  211.0 0.1 compare_select_fusion
  211.1 0.3 fusion.5
  211.5 64.2 %psum.7 = f32[2,512]{1,0:T(2,128)S(1)} all-reduce(f32[2,512]{1,0:T(2,128)S(1)} %pad_maximum_fusion), channel_id=1, replica_groups=mesh['dp'=4,'expert'=32] {'dp','expert'}, use_global_device_ids=true, to_apply=%region_9.10 | all-reduce | flops 1024 | bytes 8192 | tf_op jit(solution)/shard_map/psum | solution.py:291
  275.7 0.6 slice_reduce_fusion.1
  276.3 0.1 constant_dynamic-slice_fusion.1
  277.0 0.5 subtract_bitcast_fusion
  (45 shorter events, 0.5 us)
Async XLA Ops:
  7.2 145.1 %all-gather.3.cloned.1.call-start = ((), (), s32[]{:S(2)}) async-start(), calls=%async_computation.1 | async-start | bytes 17301504 | tf_op jit(solution)/shard_map/all_gather | solution.py:274
  7.2 2.2 copy-start
  9.4 1.0 copy-start.1
  10.4 0.9 copy-start.2
  11.3 0.7 copy-start.3
  12.0 0.7 copy-start.4
  12.7 0.7 copy-start.5
  13.4 65.5 %copy-start.7 = (s32[256]{0:T(256)S(1)}, s32[256]{0:T(256)}, u32[]{:S(2)}) copy-start(s32[256]{0:T(256)} %param.21) | copy-start | bytes 3076
  13.4 66.0 %copy-start.6 = (s32[256]{0:T(256)S(1)}, s32[256]{0:T(256)}, u32[]{:S(2)}) copy-start(s32[256]{0:T(256)} %param.22) | copy-start | bytes 3076
  13.4 138.8 %copy-start.9 = (bf16[1024,1024]{1,0:T(8,128)(2,1)S(1)}, bf16[1024,1024]{1,0:T(8,128)(2,1)}, u32[]{:S(2)}) copy-start(bf16[1024,1024]{1,0:T(8,128)(2,1)} %param.20) | copy-start | bytes 6291460
  81.3 4.8 %collective-permute-start = (s32[2]{0:T(128)S(1)}, s32[2]{0:T(128)S(1)}, u32[]{:S(2)}, u32[]{:S(2)}) collective-permute-start(s32[2]{0:T(128)S(1)} %pad_add_fusion.1), channel_id=1, source_target_pairs={{1,0},{2,1},{3,2},{4,3},{5,4},{6,5},{7,6},{8,7},{9,8},{10,9},{11,1... | collective-permute-start | bytes 32 | tf_op jit(solution)/shard_map/ppermute | solution.py:268
  197.8 13.1 %all-to-all-start = ((f32[32,3,256]{2,1,0:T(4,128)}), f32[32,3,256]{2,1,0:T(4,128)S(1)}, u32[]{:S(2)}, u32[]{:S(2)}) async-start(f32[32,3,256]{2,1,0:T(4,128)} %copy.20), calls=%async_computation | async-start | bytes 262144 | tf_op jit(solution)/shard_map/all_to_all | solution.py:282
  211.1 66.4 %copy-start.8 = (f32[256]{0:T(256)}, f32[256]{0:T(256)S(1)}, u32[]{:S(2)}) copy-start(f32[256]{0:T(256)S(1)} %compare_select_fusion) | copy-start | bytes 3076
Sparse Core Ops, SparseCore 0:
  79.0 73.1 all-gather.2

commit v2 on v1

v2 whole, which is shorter than its diff:
```python
import jax
import jax.numpy as jnp
from jax import lax
from jax.experimental import pallas as pl
from jax.experimental.pallas import tpu as pltpu
from jax.sharding import PartitionSpec as P

TOP = 2
DOC_DEV = 4
SIDE = 4
DP = 4
OWNERS = 32
GROUPS = 4
PEERS = 16
BOTH = ("dp", "expert")
EPSILON = 1e-06
MESH_ID = pl.DeviceIdType.MESH
STEP_SLOT = (0, 0, 4, 3, 1, 4, 3, 1, 2, 2, 5, 7, 6, 5, 7, 6)
STEP_HALF = (0, 1, 0, 0, 0, 1, 1, 1, 0, 1, 0, 0, 0, 1, 1, 1)


def normalize(values, gain_vector):
    inv_scale = lax.rsqrt(jnp.mean(values * values, axis=-1, keepdims=True) + EPSILON)
    return values * inv_scale * gain_vector


def looked_up(table, step):
    found = jnp.int32(table[0])
    for k in range(1, len(table)):
        found = jnp.where(step == k, jnp.int32(table[k]), found)
    return found


def kernel(
    hidden_hbm, gain_ref, router_ref, routes_ref, final_gain_ref, tokens_ref, docs_ref,
    gate_hbm, up_hbm, down_hbm, vocab_hbm,
    loss_ref, score_ref,
    hidden, normed, outgoing, arrived, gate_w, up_w, down_w, result, returned, place_a, place_b, mixed,
    own_raw, other_raw, vocab_t, rows, ids, next_ids, targets, stats_out, stats_in, sums_out, sums_in, lead_in,
    dp_out, dp_in,
    load_sem, self_sem, send_out, recv_out, send_back, recv_back, send_voc, recv_voc, send_ids, recv_ids,
    send_tgt, recv_tgt, send_rows, recv_rows, send_stats, recv_stats, send_sums, recv_sums, send_lead, recv_lead,
    send_dp, recv_dp,
):
    tokens, width = hidden.shape
    local = gate_hbm.shape[0]
    experts = OWNERS * local
    slots = outgoing.shape[2]
    part = local * slots
    per_group = OWNERS // GROUPS
    chunk = per_group * slots
    voc = vocab_hbm.shape[1]
    quarter = voc // DP
    half = tokens // 2
    dp = lax.axis_index("dp")
    own = lax.axis_index("expert")
    x, z, core = own // 8, (own // 2) % SIDE, own % 2
    linear = dp * OWNERS + own
    devices = DP * OWNERS
    mate_x = x + 1 - 2 * (x % 2)
    mirror = (SIDE - 1 - x) * 8 + z * 2 + core

    def at(device, plane=dp):
        return {"dp": plane, "expert": device}

    def shifted(steps):
        other = (linear + steps + devices) % devices
        return at(other % OWNERS, other // OWNERS)

    def partner(i, sign):
        dx = (i % 8) // 2
        dz = (i // 8 + SIDE - dx) % SIDE
        dc = i % 2
        return ((x + sign * dx + SIDE) % SIDE) * 8 + ((z + sign * dz + SIDE) % SIDE) * 2 + (core + dc) % 2

    def peer(q):
        jx, jz, jc = q // 8, (q // 2) % SIDE, q % 2
        return (x + jx * (mate_x - x)) * 8 + ((z + jz) % SIDE) * 2 + (core + jc) % 2

    def seen_from(q):
        return (q // 8) * 8 + ((SIDE - (q // 2) % SIDE) % SIDE) * 2 + q % 2

    def remote(source, target, send, recv, device):
        return pltpu.make_async_remote_copy(
            src_ref=source, dst_ref=target, send_sem=send, recv_sem=recv, device_id=device, device_id_type=MESH_ID
        )

    barrier = pltpu.get_barrier_semaphore()

    @pl.loop(1, OWNERS)
    def _(i):
        pl.semaphore_signal(barrier, inc=1, device_id=at(partner(i, 1)), device_id_type=MESH_ID)

    for dy in range(1, DP):
        pl.semaphore_signal(barrier, inc=1, device_id=at(own, (dp + dy) % DP), device_id_type=MESH_ID)
    for steps in (-1, 1):
        pl.semaphore_signal(barrier, inc=1, device_id=shifted(steps), device_id_type=MESH_ID)

    loads = []
    for n, (source, target) in enumerate(
        (
            (hidden_hbm, hidden),
            (gate_hbm, gate_w),
            (up_hbm, up_w),
            (down_hbm, down_w),
            (vocab_hbm, own_raw),
        )
    ):
        copy = pltpu.make_async_copy(source, target, load_sem.at[n])
        copy.start()
        loads.append(copy)

    ids[...] = jnp.zeros_like(ids)
    ids[0:2, :] = tokens_ref[...]
    ids[2:4, :] = docs_ref[...]
    pl.semaphore_wait(barrier, OWNERS - 1 + DP - 1 + 2)

    def columns(plane):
        return pl.ds(pl.multiple_of(plane * quarter, quarter), quarter)

    def voc_across():
        return remote(
            vocab_hbm.at[:, columns(dp)], other_raw.at[:, columns(dp)], send_voc.at[0], recv_voc.at[0], at(mirror)
        )

    def voc_along(dy, source):
        return remote(
            other_raw.at[:, columns(source)], other_raw.at[:, columns(source)], send_voc.at[dy], recv_voc.at[dy],
            at(own, (dp + dy) % DP),
        )

    def ids_copy():
        return remote(ids, next_ids, send_ids, recv_ids, shifted(-1))

    ids_copy().start()
    voc_across().start()

    loads[0].wait()
    normed[...] = normalize(hidden[...].astype(jnp.float32), gain_ref[...]).astype(jnp.bfloat16)
    first = routes_ref[0:1, :]
    second = routes_ref[1:2, :]
    expert_iota = lax.broadcasted_iota(jnp.int32, (experts, tokens), 0)
    is_first = expert_iota == first
    is_second = expert_iota == second
    member = jnp.where(is_first | is_second, 1.0, 0.0).astype(jnp.bfloat16)
    earlier = (
        lax.broadcasted_iota(jnp.int32, (tokens, tokens), 0) < lax.broadcasted_iota(jnp.int32, (tokens, tokens), 1)
    )
    rank = jnp.dot(
        member, jnp.where(earlier, 1.0, 0.0).astype(jnp.bfloat16), preferred_element_type=jnp.float32
    )

    def position(expert, chosen):
        owner = expert // local
        dx = (owner // 8 + SIDE - x) % SIDE
        dz = ((owner // 2) % SIDE + SIDE - z) % SIDE
        dc = (owner + core) % 2
        index = ((dx + dz) % SIDE) * 8 + dx * 2 + dc
        own_rank = jnp.sum(jnp.where(chosen, rank, 0.0), axis=0, keepdims=True).astype(jnp.int32)
        return index * part + (expert % local) * slots + own_rank

    first_pos = position(first, is_first)
    second_pos = position(second, is_second)

    def slot_rows(i):
        return pl.ds(pl.multiple_of(i * slots, slots), slots)

    def out(i):
        return remote(
            outgoing.at[i], arrived.at[:, slot_rows(i)], send_out.at[i], recv_out.at[i], at(partner(i, 1))
        )

    def back(i):
        return remote(
            result.at[:, slot_rows(i)], returned.at[i], send_back.at[i], recv_back.at[i], at(partner(i, -1))
        )

    for group in range(GROUPS):
        slot_iota = lax.broadcasted_iota(jnp.int32, (per_group * part, tokens), 0) + group * per_group * part
        chosen = (slot_iota == first_pos) | (slot_iota == second_pos)
        block = jnp.dot(
            jnp.where(chosen, 1.0, 0.0).astype(jnp.bfloat16), normed[...], preferred_element_type=jnp.float32
        )
        outgoing[pl.ds(group * per_group, per_group)] = block.astype(jnp.bfloat16).reshape(
            per_group, local, slots, width
        )
        if group == 0:
            own_copy = pltpu.make_async_copy(outgoing.at[0], arrived.at[:, pl.ds(0, slots)], self_sem)
            own_copy.start()

        @pl.loop(max(1, group * per_group), (group + 1) * per_group)
        def _(i):
            out(i).start()

    ids_copy().wait_recv()
    row_iota = lax.broadcasted_iota(jnp.int32, ids.shape, 0)
    lane_iota = lax.broadcasted_iota(jnp.int32, ids.shape, 1)
    own_ids = ids[...]
    after = pltpu.roll(own_ids, half - 1, 1)
    ends = lane_iota == half - 1
    after = jnp.where(ends & (row_iota == 0), own_ids[1:2, 0:1], after)
    after = jnp.where(ends & (row_iota == 1), next_ids[0:1, 0:1], after)
    after = jnp.where(ends & (row_iota == 2), own_ids[3:4, 0:1], after)
    after = jnp.where(ends & (row_iota == 3), next_ids[2:3, 0:1], after)
    targets[0] = after

    def target_copy(q):
        there = seen_from(q)
        return remote(targets.at[0], targets.at[there], send_tgt.at[q], recv_tgt.at[there], at(peer(q)))

    @pl.loop(1, PEERS)
    def _(q):
        target_copy(q).start()

    router_scores = lax.dot_general(
        router_ref[...], normed[...], (((1,), (1,)), ((), ())), preferred_element_type=jnp.float32
    )
    picked = jnp.sum(
        jnp.where(is_first, router_scores, 0.0) - jnp.where(is_second, router_scores, 0.0), axis=0, keepdims=True
    )
    first_gate = jax.nn.sigmoid(picked)
    lines = lax.broadcasted_iota(jnp.int32, (128, tokens), 0)
    table = jnp.where(
        lines == 0,
        first_pos.astype(jnp.float32),
        jnp.where(lines == 1, second_pos.astype(jnp.float32), jnp.where(lines == 2, first_gate, 0.0)),
    )
    per_token = table.T
    place_iota = lax.broadcasted_iota(jnp.int32, (tokens, experts * slots), 1).astype(jnp.float32)
    place_a[...] = jnp.where(place_iota == per_token[:, 0:1], 1.0, 0.0).astype(jnp.bfloat16)
    place_b[...] = jnp.where(place_iota == per_token[:, 1:2], 1.0, 0.0).astype(jnp.bfloat16)
    gate_a = per_token[:, 2:3]
    gate_b = 1.0 - gate_a

    loads[4].wait()

    @pl.loop(0, voc // 128)
    def _(j):
        strip = pl.ds(pl.multiple_of(j * 128, 128), 128)
        vocab_t[strip, :] = own_raw[:, strip].T

    voc_across().wait_recv()
    for dy in range(1, DP):
        voc_along(dy, dp).start()

    own_copy.wait()
    for copy in loads[1:4]:
        copy.wait()

    for group in range(GROUPS):
        low, high = max(1, group * per_group), (group + 1) * per_group

        @pl.loop(low, high)
        def _(i):
            out(i).wait_recv()

        @pl.loop(0, local)
        def _(n):
            inputs = arrived[n, pl.ds(group * chunk, chunk)]
            gate_part = jnp.dot(inputs, gate_w[n], preferred_element_type=jnp.float32)
            up_part = jnp.dot(inputs, up_w[n], preferred_element_type=jnp.float32)
            active = (jax.nn.silu(gate_part) * up_part).astype(jnp.bfloat16)
            result[n, pl.ds(group * chunk, chunk)] = jnp.dot(
                active, down_w[n], preferred_element_type=jnp.float32
            ).astype(jnp.bfloat16)

        if group == 0:
            home = pltpu.make_async_copy(result.at[:, pl.ds(0, slots)], returned.at[0], self_sem)
            home.start()

        @pl.loop(low, high)
        def _(i):
            back(i).start()

    for dy in range(DP):
        source = (dp + DP - dy) % DP
        if dy:
            voc_along(dy, source).wait_recv()

        @pl.loop(0, quarter // 128)
        def _(j):
            start = source * quarter + j * 128
            vocab_t[pl.ds(pl.multiple_of(voc + start, 128), 128), :] = other_raw[
                :, pl.ds(pl.multiple_of(start, 128), 128)
            ].T

    home.wait()
    mixed[...] = hidden[...].astype(jnp.float32)
    for group in range(GROUPS):
        low, high = max(1, group * per_group), (group + 1) * per_group

        @pl.loop(low, high)
        def _(i):
            back(i).wait_recv()

        block = returned[pl.ds(group * per_group, per_group)].reshape(per_group * part, width)
        span = slice(group * per_group * part, (group + 1) * per_group * part)
        mixed[...] += gate_a * jnp.dot(
            place_a[:, span], block, preferred_element_type=jnp.float32
        ) + gate_b * jnp.dot(place_b[:, span], block, preferred_element_type=jnp.float32)
    final_rows = normalize(mixed[...], final_gain_ref[...]).astype(jnp.bfloat16)
    rows[0, 0, 0] = final_rows[:half]
    rows[0, 1, 0] = final_rows[half:]

    above = x * 8 + ((z + 1) % SIDE) * 2 + core
    below = x * 8 + ((z + SIDE - 1) % SIDE) * 2 + core
    mate = mate_x * 8 + z * 2 + core
    sibling = x * 8 + z * 2 + 1 - core
    sends = []

    def row_copy(slot, h, there, device, side=0):
        number = len(sends)

        def made():
            return remote(
                rows.at[slot, h, 0], rows.at[there, h, side], send_rows.at[number],
                recv_rows.at[(there * 2 + h) * 2 + side], at(device),
            )

        sends.append(made)
        return made

    def row_arrival(slot, h, side):
        return remote(
            rows.at[slot, h, side], rows.at[slot, h, side], send_rows.at[0],
            recv_rows.at[(slot * 2 + h) * 2 + side], at(sibling),
        )

    onward = {}
    for h in range(2):
        onward[0, h] = [
            row_copy(0, h, 3, above), row_copy(0, h, 1, below), row_copy(0, h, 4, mate), row_copy(0, h, 0, sibling, 1)
        ]
        onward[4, h] = [row_copy(4, h, 7, above), row_copy(4, h, 5, below)]
        onward[3, h] = [row_copy(3, 0, 2, above)] if h == 0 else []
        onward[1, h] = [row_copy(1, 1, 2, below)] if h == 1 else []
        onward[2, h] = [row_copy(2, h, 6, mate)]
        for slot in range(1, 8):
            onward.setdefault((slot, h), []).append(row_copy(slot, h, slot, sibling, 1))
    for h in range(2):
        for made in onward[0, h]:
            made().start()

    @pl.loop(1, PEERS)
    def _(q):
        target_copy(seen_from(q)).wait_recv()

    own_base = own * voc
    other_base = mirror * voc
    tile = voc // 2

    def stats_copy(q):
        there = seen_from(q)
        return remote(stats_out.at[q], stats_in.at[there], send_stats.at[q], recv_stats.at[there], at(peer(q)))

    @pl.loop(0, PEERS)
    def _(q):
        stats_out[q] = jnp.zeros(stats_out.shape[1:], jnp.float32)

    @pl.loop(0, len(STEP_SLOT))
    def _(step):
        slot = looked_up(STEP_SLOT, step)
        h = looked_up(STEP_HALF, step)
        for k in range(2, len(STEP_SLOT)):

            @pl.when(step == k)
            def _():
                row_arrival(STEP_SLOT[k], STEP_HALF[k], 0).wait_recv()
                for made in onward[STEP_SLOT[k], STEP_HALF[k]]:
                    made().start()

        row_arrival(slot, h, 1).wait_recv()
        block = rows[slot, h].reshape(2 * half, width)
        wanted = jnp.concatenate(
            [targets[2 * slot, pl.ds(h, 1), :], targets[2 * slot + 1, pl.ds(h, 1), :]], axis=1
        )
        high = total = hit = None
        for n in range(4):
            scores = lax.dot_general(
                vocab_t[n * tile : (n + 1) * tile, :], block, (((1,), (1,)), ((), ())),
                preferred_element_type=jnp.float32,
            )
            base = (own_base if n < 2 else other_base) + (n % 2) * tile
            match = lax.broadcasted_iota(jnp.int32, scores.shape, 0) == wanted - base
            stacked = scores.reshape(tile // 8, 8, 2 * half)
            found = jnp.sum(jnp.where(match, scores, 0.0).reshape(stacked.shape), axis=0)
            top = jnp.max(stacked, axis=0)
            if n:
                top = jnp.maximum(top, high)
            summed = jnp.sum(jnp.exp(stacked - top[None]), axis=0)
            if n:
                summed = summed + total * jnp.exp(high - top)
                found = found + hit
            high, total, hit = top, summed, found
        top = jnp.max(high, axis=0, keepdims=True)
        summed = jnp.sum(total * jnp.exp(high - top), axis=0, keepdims=True)
        found = jnp.sum(hit, axis=0, keepdims=True)
        for side in range(2):
            lanes = slice(side * half, (side + 1) * half)
            stats_out[2 * slot + side, pl.ds(h, 1), :] = top[:, lanes]
            stats_out[2 * slot + side, pl.ds(2 + h, 1), :] = summed[:, lanes]
            stats_out[2 * slot + side, pl.ds(4 + h, 1), :] = found[:, lanes]

        @pl.when(h == 1)
        def _():
            @pl.when(slot > 0)
            def _():
                stats_copy(2 * slot).start()

            stats_copy(2 * slot + 1).start()

    stats_in[0] = stats_out[0]

    @pl.loop(1, PEERS)
    def _(q):
        stats_copy(seen_from(q)).wait_recv()

    every = stats_in[...]
    top = jnp.max(every[:, 0:2], axis=0)
    summed = jnp.sum(every[:, 2:4] * jnp.exp(every[:, 0:2] - top[None]), axis=0)
    found = jnp.sum(every[:, 4:6], axis=0)
    docs = docs_ref[...]
    two_rows = lax.broadcasted_iota(jnp.int32, docs.shape, 0)
    two_lanes = lax.broadcasted_iota(jnp.int32, docs.shape, 1)
    at_end = (two_rows == 1) & (two_lanes == half - 1) & (linear == devices - 1)
    counted = (targets[0, 2:4, :] == docs) & jnp.logical_not(at_end)
    token_loss = jnp.where(counted, top + jnp.log(summed) - found, 0.0)
    loss_ref[...] = token_loss

    def whole(values):
        return jnp.sum(jnp.sum(values, axis=1, keepdims=True), axis=0, keepdims=True)

    def of_document(number):
        mask = docs == number
        return whole(jnp.where(mask, token_loss, 0.0)), whole(jnp.where(mask, 1.0, 0.0))

    lead_loss, lead_length = of_document(DOC_DEV * linear - 1)
    lines = lax.broadcasted_iota(jnp.int32, (8, 128), 0)
    sums_out[...] = jnp.where(
        lines == 0, whole(token_loss), jnp.where(lines == 1, lead_loss, jnp.where(lines == 2, lead_length, 0.0))
    )

    def sum_copy(i):
        return remote(sums_out, sums_in.at[i], send_sums.at[i], recv_sums.at[i], at(partner(i, 1)))

    def lead_copy():
        return remote(sums_out, lead_in, send_lead, recv_lead, shifted(-1))

    @pl.loop(1, OWNERS)
    def _(i):
        sum_copy(i).start()

    lead_copy().start()
    sums_in[0] = sums_out[...]
    parts = [of_document(DOC_DEV * linear + j) for j in range(DOC_DEV)]

    @pl.loop(1, OWNERS)
    def _(i):
        sum_copy(i).wait_recv()

    dp_out[...] = jnp.sum(sums_in[...], axis=0)

    def dp_copy(dy):
        return remote(dp_out, dp_in.at[dy], send_dp.at[dy], recv_dp.at[dy], at(own, (dp + dy) % DP))

    for dy in range(1, DP):
        dp_copy(dy).start()
    lead_copy().wait_recv()
    dp_in[0] = dp_out[...]
    for dy in range(1, DP):
        dp_copy(dy).wait_recv()
    global_sum = jnp.sum(dp_in[...], axis=0)[0:1, 0:1]
    global_mean = global_sum / (tokens * devices - DOC_DEV * devices)
    lanes = lax.broadcasted_iota(jnp.int32, (1, 128), 1)
    scores = jnp.zeros((1, 128), jnp.float32)
    for j, (part_loss, part_length) in enumerate(parts):
        if j == DOC_DEV - 1:
            part_loss = part_loss + lead_in[1:2, 0:1]
            part_length = part_length + lead_in[2:3, 0:1]
        scores = jnp.where(lanes == j, part_loss / part_length - global_mean, scores)
    score_ref[...] = scores[:, 0:DOC_DEV]

    @pl.loop(1, OWNERS)
    def _(i):
        out(i).wait_send()
        back(i).wait_send()
        sum_copy(i).wait_send()

    @pl.loop(1, PEERS)
    def _(q):
        target_copy(q).wait_send()
        stats_copy(q).wait_send()

    voc_across().wait_send()
    ids_copy().wait_send()
    lead_copy().wait_send()
    for dy in range(1, DP):
        voc_along(dy, dp).wait_send()
        dp_copy(dy).wait_send()
    for made in sends:
        made().wait_send()


def local(
    hidden_in, moe_gain, router_weight, expert_gate, expert_up, expert_down, final_gain, vocab_weight,
    token_ids, doc_ids, routes,
):
    tokens, width = hidden_in.shape
    here, _, hidden_units = expert_gate.shape
    voc = vocab_weight.shape[1]
    experts = OWNERS * here
    slots = max(2, 2 * TOP * tokens // experts)
    half = tokens // 2
    bf16, f32, i32 = jnp.bfloat16, jnp.float32, jnp.int32
    vmem = pl.BlockSpec(memory_space=pltpu.VMEM)
    hbm = pl.BlockSpec(memory_space=pl.ANY)
    dma = pltpu.SemaphoreType.DMA
    loss, score = pl.pallas_call(
        kernel,
        out_shape=(jax.ShapeDtypeStruct((2, half), f32), jax.ShapeDtypeStruct((1, DOC_DEV), f32)),
        in_specs=[hbm] + [vmem] * 6 + [hbm] * 4,
        out_specs=(vmem, vmem),
        scratch_shapes=[
            pltpu.VMEM((tokens, width), bf16),
            pltpu.VMEM((tokens, width), bf16),
            pltpu.VMEM((OWNERS, here, slots, width), bf16),
            pltpu.VMEM((here, OWNERS * slots, width), bf16),
            pltpu.VMEM((here, width, hidden_units), bf16),
            pltpu.VMEM((here, width, hidden_units), bf16),
            pltpu.VMEM((here, hidden_units, width), bf16),
            pltpu.VMEM((here, OWNERS * slots, width), bf16),
            pltpu.VMEM((OWNERS, here, slots, width), bf16),
            pltpu.VMEM((tokens, experts * slots), bf16),
            pltpu.VMEM((tokens, experts * slots), bf16),
            pltpu.VMEM((tokens, width), f32),
            pltpu.VMEM((width, voc), bf16),
            pltpu.VMEM((width, voc), bf16),
            pltpu.VMEM((2 * voc, width), bf16),
            pltpu.VMEM((8, 2, 2, half, width), bf16),
            pltpu.VMEM((8, half), i32),
            pltpu.VMEM((8, half), i32),
            pltpu.VMEM((PEERS, 8, half), i32),
            pltpu.VMEM((PEERS, 8, half), f32),
            pltpu.VMEM((PEERS, 8, half), f32),
            pltpu.VMEM((8, 128), f32),
            pltpu.VMEM((OWNERS, 8, 128), f32),
            pltpu.VMEM((8, 128), f32),
            pltpu.VMEM((8, 128), f32),
            pltpu.VMEM((DP, 8, 128), f32),
            dma((5,)),
            dma,
            dma((OWNERS,)),
            dma((OWNERS,)),
            dma((OWNERS,)),
            dma((OWNERS,)),
            dma((DP,)),
            dma((DP,)),
            dma,
            dma,
            dma((PEERS,)),
            dma((PEERS,)),
            dma((32,)),
            dma((32,)),
            dma((PEERS,)),
            dma((PEERS,)),
            dma((OWNERS,)),
            dma((OWNERS,)),
            dma,
            dma,
            dma((DP,)),
            dma((DP,)),
        ],
        compiler_params=pltpu.CompilerParams(
            collective_id=0, has_side_effects=True, vmem_limit_bytes=58 * 2**20
        ),
        name="scoring",
    )(
        hidden_in, moe_gain.reshape(1, width), router_weight.T, routes.T, final_gain.reshape(1, width),
        token_ids.reshape(2, half), doc_ids.reshape(2, half), expert_gate, expert_up, expert_down, vocab_weight,
    )
    return loss.reshape(tokens), score.reshape(DOC_DEV)


def solution(mesh):
    in_specs = (
        P(BOTH, None), P(), P(), P("expert", None, None), P("expert", None, None), P("expert", None, None), P(),
        P(None, "expert"), P(BOTH), P(BOTH), P(BOTH, None),
    )
    return jax.shard_map(local, mesh=mesh, in_specs=in_specs, out_specs=(P(BOTH), P(BOTH)), check_vma=False)
```

time: 285 us -> 149 us (0.52)
  blocking collectives: 89.1 us -> 0 us
  Pallas kernels: 65.5 us -> 146 us
  waiting for transfers between devices: 48.7 us -> 0 us
  matrix products: 33.1 us -> 0 us
  other arithmetic: 15.2 us -> 0 us
  between operations: 15.4 us -> 0.64 us
  starting transfers between devices: 8.17 us -> 0 us
  local copies, waits for them, and re-layouts: 8.91 us -> 2.36 us
    pallas_call x1, Pallas kernels: 65.5 us -> 146 us  [local(): pl.pallas_call(kernel, out_shape=(jax.ShapeDtypeStruct((2, half), f32), j...]
    psum x1 -> x0, blocking collectives: 64.2 us -> none  [local(): whole = lax.psum(partial, BOTH)]
    all_gather x1 -> x0, waiting for transfers between devices: 39.8 us -> none  [local(): all_rows = lax.all_gather(final_rows, 'expert', axis=0, tiled=True)]
    dot_general x9 -> x0, matrix products: 33.1 us -> none  [the longest x8 32.8 us: stats_block(): jnp.dot(hidden_rows, vocab_weight, preferred_element_type=jnp.float32)]
    all_gather x1 -> x0, blocking collectives: 24.9 us -> none  [local(): all_targets = lax.all_gather(targets, 'expert', axis=0, tiled=True)]
    reduce_sum x11 -> x0, other arithmetic: 12 us -> none  [the longest x8 11.3 us: stats_block(): totals = jnp.sum(jnp.exp(scores - highest[:, None]), axis=1)]
    all_to_all x1 -> x0, waiting for transfers between devices: 7 us -> none  [local(): lax.all_to_all(stats, 'expert', split_axis=0, concat_axis=0, tiled=True)]
    all_to_all x1 -> x0, starting transfers between devices: 5.38 us -> none  [local(): lax.all_to_all(stats, 'expert', split_axis=0, concat_axis=0, tiled=True)]
  transfers between devices with their start and end apart: 3 -> 0, of which waited for: 3 -> 0; matrix products, arithmetic and copies ran while one was open for 1% -> 0% of each run, Pallas kernels for 0% -> 0%
where the time goes in v2:
time: 149 us
  Pallas kernels  146 us (98%)
  local copies, waits for them, and re-layouts  2.36 us (2%)
    pallas_call x1, Pallas kernels, local(): pl.pallas_call(kernel, out_shape=(jax.ShapeDtypeStruct((2, half), f32), j...  146 us

profile of v2, /device:TPU:1, one launch (start us, length us, event | category | flops | bytes accessed | tf_op | source)
XLA Modules:
  0.0 149.1 jit_solution(5927036031619895576)
XLA Ops:
  0.6 146.1 %scoring.1 = (f32[2,128]{1,0:T(2,128)}, f32[1,4]{1,0:T(1,128)}) custom-call(bf16[256,1024]{1,0:T(8,128)(2,1)} %hidden_hbm.1, f32[1,1024]{1,0:T(1,128)} %bitcast.9, bf16[64,1024]{1,0:T(8,128)(2,1)} %bitcast.8, s32[2,256]{1,0:T(2,128)} %bitcast.11, f32[1,1024]{1,0:T(1,128)} %bitcast.10, s32[2,128]{1,0:T(2,128)} %bitcast.12, s32[2,128]{1,0:T(2,128)} %bitcast.13, ...), custom_call_target="tpu_custom_call" | custom-call | tf_op jit(solution)/shard_map/scoring/pallas_call | solution.py:518
  146.7 1.2 copy.15
  148.0 1.1 copy.16

commit v3 on v2

v3 whole, which is shorter than its diff:
```python
import jax
import jax.numpy as jnp
from jax import lax
from jax.experimental import pallas as pl
from jax.experimental.pallas import tpu as pltpu
from jax.sharding import PartitionSpec as P
TOP = 2
DOC_DEV = 4
SIDE = 4
DP = 4
OWNERS = 32
GROUPS = 4
PEERS = 16
BOTH = ('dp', 'expert')
ABOVE, BELOW, MATE, SIBLING = ("above", "below", "mate", "sibling")
FIRST_SENDS = (
    (0, 0, ABOVE), (0, 0, BELOW), (0, 0, MATE), (0, 0, SIBLING), (0, 1, ABOVE), (0, 1, BELOW), (0, 1, MATE), (0, 1, SIBLING),
)
SCHEDULE = (
    ((0, 0), (1, 0), (4, 0), (1, 0, BELOW), (4, 0, SIBLING), (1, 0, MATE), (4, 0, ABOVE),),
    ((4, 0),),
    ((0, 1),),
    ((4, 1), (1, 1), (4, 1), (1, 1, SIBLING), (3, 1), (1, 1, BELOW), (3, 0), (4, 1, SIBLING), (3, 1, MATE), (4, 1, BELOW), (3, 1, SIBLING),),
    ((1, 1),),
    ((3, 1), (5, 0), (3, 0, SIBLING), (7, 0), (7, 0, ABOVE), (1, 0, SIBLING), (7, 0, SIBLING), (5, 0, SIBLING),),
    ((7, 0),),
    ((3, 0), (2, 0), (2, 0, SIBLING),),
    ((2, 0), (2, 1), (2, 1, MATE), (7, 1), (2, 1, SIBLING),),
    ((1, 0),),
    ((5, 0), (6, 0),),
    ((2, 1), (6, 0, SIBLING),),
    ((6, 0), (7, 1, SIBLING), (5, 1),),
    ((7, 1), (6, 1), (5, 1, SIBLING), (6, 1, SIBLING),),
    ((6, 1),),
    ((5, 1),),
)
EPSILON = 1e-06
MESH_ID = pl.DeviceIdType.MESH
EPSILON = 1e-06

def normalize(values, gain_vector):
    inv_scale = lax.rsqrt(jnp.mean(values * values, axis=-1, keepdims=True) + EPSILON)
    return values * inv_scale * gain_vector

def looked_up(table, step):
    found = jnp.int32(table[0])
    for k in range(1, len(table)):
        found = jnp.where(step == k, jnp.int32(table[k]), found)
    return found

def kernel(hidden_hbm, gain_ref, router_ref, routes_ref, final_gain_ref, tokens_ref, docs_ref, gate_hbm, up_hbm, down_hbm, vocab_hbm, made_ref, hidden, normed, outgoing, arrived, gate_w, up_w, down_w, result, returned, place_a, place_b, mixed, own_raw, other_raw, vocab_t, rows, ids, next_ids, targets, stats_out, stats_in, sums_out, sums_in, lead_in, wide_out, wide_in, load_sem, self_sem, send_out, recv_out, send_back, recv_back, send_voc, recv_voc, send_ids, recv_ids, send_tgt, recv_tgt, send_rows, recv_rows, send_stats, recv_stats, send_sums, recv_sums, send_lead, recv_lead, send_wide, recv_wide):
    tokens, width = hidden.shape
    local = gate_hbm.shape[0]
    experts = OWNERS * local
    slots = outgoing.shape[2]
    part = local * slots
    per_group = OWNERS // GROUPS
    chunk = per_group * slots
    voc = vocab_hbm.shape[1]
    quarter = voc // DP
    half = tokens // 2
    dp = lax.axis_index('dp')
    own = lax.axis_index('expert')
    x, z, core = (own // 8, own // 2 % SIDE, own % 2)
    linear = dp * OWNERS + own
    devices = DP * OWNERS
    mate_x = x + 1 - 2 * (x % 2)
    mirror = (SIDE - 1 - x) * 8 + z * 2 + core

    def at(device, plane=dp):
        return {'dp': plane, 'expert': device}

    def shifted(steps):
        other = (linear + steps + devices) % devices
        return at(other % OWNERS, other // OWNERS)

    def partner(i, sign):
        dx = i % 8 // 2
        dz = (i // 8 + SIDE - dx) % SIDE
        dc = i % 2
        return (x + sign * dx + SIDE) % SIDE * 8 + (z + sign * dz + SIDE) % SIDE * 2 + (core + dc) % 2

    def peer(q):
        jx, jz, jc = (q // 8, q // 2 % SIDE, q % 2)
        return (x + jx * (mate_x - x)) * 8 + (z + jz) % SIDE * 2 + (core + jc) % 2

    def seen_from(q):
        return q // 8 * 8 + (SIDE - q // 2 % SIDE) % SIDE * 2 + q % 2

    def across(i):
        return (own if i % 2 == 0 else mirror, (dp + i // 2) % DP)

    def remote(source, target, send, recv, device):
        return pltpu.make_async_remote_copy(src_ref=source, dst_ref=target, send_sem=send, recv_sem=recv, device_id=device, device_id_type=MESH_ID)
    barrier = pltpu.get_barrier_semaphore()

    @pl.loop(1, OWNERS)
    def _(i):
        pl.semaphore_signal(barrier, inc=1, device_id=at(partner(i, 1)), device_id_type=MESH_ID)
    for i in range(2, 2 * DP):
        device, plane = across(i)
        pl.semaphore_signal(barrier, inc=1, device_id=at(device, plane), device_id_type=MESH_ID)
    for steps in (-1, 1):
        pl.semaphore_signal(barrier, inc=1, device_id=shifted(steps), device_id_type=MESH_ID)
    loads = []
    for n, (source, target) in enumerate(((hidden_hbm, hidden), (gate_hbm, gate_w), (up_hbm, up_w), (down_hbm, down_w), (vocab_hbm, own_raw))):
        copy = pltpu.make_async_copy(source, target, load_sem.at[n])
        copy.start()
        loads.append(copy)
    ids[...] = jnp.zeros_like(ids)
    ids[0:2, :] = tokens_ref[...]
    ids[2:4, :] = docs_ref[...]
    pl.semaphore_wait(barrier, OWNERS - 1 + 2 * (DP - 1) + 2)

    def columns(plane):
        return pl.ds(pl.multiple_of(plane * quarter, quarter), quarter)

    def voc_across(piece):
        span = pl.ds(pl.multiple_of(dp * quarter + piece * (quarter // 2), quarter // 2), quarter // 2)
        n = piece * DP
        return remote(vocab_hbm.at[:, span], other_raw.at[:, span], send_voc.at[n], recv_voc.at[n], at(mirror))

    def voc_along(dy, source):
        return remote(other_raw.at[:, columns(source)], other_raw.at[:, columns(source)], send_voc.at[dy], recv_voc.at[dy], at(own, (dp + dy) % DP))

    def ids_copy():
        return remote(ids, next_ids, send_ids, recv_ids, shifted(-1))
    ids_copy().start()
    for piece in range(2):
        voc_across(piece).start()
    loads[0].wait()
    normed[...] = normalize(hidden[...].astype(jnp.float32), gain_ref[...]).astype(jnp.bfloat16)
    first = routes_ref[0:1, :]
    second = routes_ref[1:2, :]
    expert_iota = lax.broadcasted_iota(jnp.int32, (experts, tokens), 0)
    is_first = expert_iota == first
    is_second = expert_iota == second
    member = jnp.where(is_first | is_second, 1.0, 0.0).astype(jnp.bfloat16)
    earlier = lax.broadcasted_iota(jnp.int32, (tokens, tokens), 0) < lax.broadcasted_iota(jnp.int32, (tokens, tokens), 1)
    rank = jnp.dot(member, jnp.where(earlier, 1.0, 0.0).astype(jnp.bfloat16), preferred_element_type=jnp.float32)

    def position(expert, chosen):
        owner = expert // local
        dx = (owner // 8 + SIDE - x) % SIDE
        dz = (owner // 2 % SIDE + SIDE - z) % SIDE
        dc = (owner + core) % 2
        index = (dx + dz) % SIDE * 8 + dx * 2 + dc
        own_rank = jnp.sum(jnp.where(chosen, rank, 0.0), axis=0, keepdims=True).astype(jnp.int32)
        return index * part + expert % local * slots + own_rank
    first_pos = position(first, is_first)
    second_pos = position(second, is_second)

    def slot_rows(i):
        return pl.ds(pl.multiple_of(i * slots, slots), slots)

    def out(i):
        return remote(outgoing.at[i], arrived.at[:, slot_rows(i)], send_out.at[i], recv_out.at[i], at(partner(i, 1)))

    def back(i):
        return remote(result.at[:, slot_rows(i)], returned.at[i], send_back.at[i], recv_back.at[i], at(partner(i, -1)))
    for group in range(GROUPS):
        slot_iota = lax.broadcasted_iota(jnp.int32, (per_group * part, tokens), 0) + group * per_group * part
        chosen = (slot_iota == first_pos) | (slot_iota == second_pos)
        block = jnp.dot(jnp.where(chosen, 1.0, 0.0).astype(jnp.bfloat16), normed[...], preferred_element_type=jnp.float32)
        outgoing[pl.ds(group * per_group, per_group)] = block.astype(jnp.bfloat16).reshape(per_group, local, slots, width)
        if group == 0:
            own_copy = pltpu.make_async_copy(outgoing.at[0], arrived.at[:, pl.ds(0, slots)], self_sem)
            own_copy.start()

        @pl.loop(max(1, group * per_group), (group + 1) * per_group)
        def _(i):
            out(i).start()
    ids_copy().wait_recv()
    row_iota = lax.broadcasted_iota(jnp.int32, ids.shape, 0)
    lane_iota = lax.broadcasted_iota(jnp.int32, ids.shape, 1)
    own_ids = ids[...]
    after = pltpu.roll(own_ids, half - 1, 1)
    ends = lane_iota == half - 1
    after = jnp.where(ends & (row_iota == 0), own_ids[1:2, 0:1], after)
    after = jnp.where(ends & (row_iota == 1), next_ids[0:1, 0:1], after)
    after = jnp.where(ends & (row_iota == 2), own_ids[3:4, 0:1], after)
    after = jnp.where(ends & (row_iota == 3), next_ids[2:3, 0:1], after)
    targets[0] = after

    def target_copy(q):
        there = seen_from(q)
        return remote(targets.at[0], targets.at[there], send_tgt.at[q], recv_tgt.at[there], at(peer(q)))

    @pl.loop(1, PEERS)
    def _(q):
        target_copy(q).start()
    router_scores = lax.dot_general(router_ref[...], normed[...], (((1,), (1,)), ((), ())), preferred_element_type=jnp.float32)
    picked = jnp.sum(jnp.where(is_first, router_scores, 0.0) - jnp.where(is_second, router_scores, 0.0), axis=0, keepdims=True)
    first_gate = jax.nn.sigmoid(picked)
    lines = lax.broadcasted_iota(jnp.int32, (128, tokens), 0)
    table = jnp.where(lines == 0, first_pos.astype(jnp.float32), jnp.where(lines == 1, second_pos.astype(jnp.float32), jnp.where(lines == 2, first_gate, 0.0)))
    per_token = table.T
    place_iota = lax.broadcasted_iota(jnp.int32, (tokens, experts * slots), 1).astype(jnp.float32)
    place_a[...] = jnp.where(place_iota == per_token[:, 0:1], 1.0, 0.0).astype(jnp.bfloat16)
    place_b[...] = jnp.where(place_iota == per_token[:, 1:2], 1.0, 0.0).astype(jnp.bfloat16)
    gate_a = per_token[:, 2:3]
    gate_b = 1.0 - gate_a
    loads[4].wait()

    @pl.loop(0, voc // 128)
    def _(j):
        strip = pl.ds(pl.multiple_of(j * 128, 128), 128)
        vocab_t[strip, :] = own_raw[:, strip].T
    voc_across(0).wait_recv()
    voc_across(1).wait_recv()
    for dy in range(1, DP):
        voc_along(dy, dp).start()
    own_copy.wait()
    for copy in loads[1:4]:
        copy.wait()
    for group in range(GROUPS):
        low, high = (max(1, group * per_group), (group + 1) * per_group)

        @pl.loop(low, high)
        def _(i):
            out(i).wait_recv()

        @pl.loop(0, local)
        def _(n):
            inputs = arrived[n, pl.ds(group * chunk, chunk)]
            gate_part = jnp.dot(inputs, gate_w[n], preferred_element_type=jnp.float32)
            up_part = jnp.dot(inputs, up_w[n], preferred_element_type=jnp.float32)
            active = (jax.nn.silu(gate_part) * up_part).astype(jnp.bfloat16)
            result[n, pl.ds(group * chunk, chunk)] = jnp.dot(active, down_w[n], preferred_element_type=jnp.float32).astype(jnp.bfloat16)
        if group == 0:
            home = pltpu.make_async_copy(result.at[:, pl.ds(0, slots)], returned.at[0], self_sem)
            home.start()

        @pl.loop(low, high)
        def _(i):
            back(i).start()
    for dy in range(DP):
        source = (dp + DP - dy) % DP
        if dy:
            voc_along(dy, source).wait_recv()

        @pl.loop(0, quarter // 128)
        def _(j):
            start = source * quarter + j * 128
            vocab_t[pl.ds(pl.multiple_of(voc + start, 128), 128), :] = other_raw[:, pl.ds(pl.multiple_of(start, 128), 128)].T
    above = x * 8 + (z + 1) % SIDE * 2 + core
    below = x * 8 + (z + SIDE - 1) % SIDE * 2 + core
    mate = mate_x * 8 + z * 2 + core
    sibling = x * 8 + z * 2 + 1 - core
    sends = []

    def row_copy(slot, h, there, device, side=0):
        number = len(sends)

        def made():
            return remote(rows.at[slot, h, 0], rows.at[there, h, side], send_rows.at[number], recv_rows.at[(there * 2 + h) * 2 + side], at(device))
        sends.append(made)
        return made

    def row_arrival(slot, h, side):
        return remote(rows.at[slot, h, side], rows.at[slot, h, side], send_rows.at[0], recv_rows.at[(slot * 2 + h) * 2 + side], at(sibling))
    copies = {}
    moves = [move for moves in (FIRST_SENDS, *(entry[1:] for entry in SCHEDULE)) for move in moves if len(move) == 3]
    for slot, h, way in moves:
        jx, jz = (slot // SIDE, slot % SIDE)
        if way == ABOVE:
            copies[slot, h, way] = row_copy(slot, h, jx * SIDE + (jz + 3) % SIDE, above)
        elif way == BELOW:
            copies[slot, h, way] = row_copy(slot, h, jx * SIDE + (jz + 1) % SIDE, below)
        elif way == MATE:
            copies[slot, h, way] = row_copy(slot, h, (1 - jx) * SIDE + jz, mate)
        else:
            copies[slot, h, way] = row_copy(slot, h, slot, sibling, 1)
    home.wait()
    mixed[...] = hidden[...].astype(jnp.float32)
    for group in range(GROUPS):
        low, high = (max(1, group * per_group), (group + 1) * per_group)

        @pl.loop(low, high)
        def _(i):
            back(i).wait_recv()
        block = returned[pl.ds(group * per_group, per_group)].reshape(per_group * part, width)
        span = slice(group * per_group * part, (group + 1) * per_group * part)

        def add(lines):
            return mixed[lines, :] + (gate_a[lines] * jnp.dot(place_a[lines, span], block, preferred_element_type=jnp.float32) + gate_b[lines] * jnp.dot(place_b[lines, span], block, preferred_element_type=jnp.float32))
        if group < GROUPS - 1:
            mixed[...] = add(slice(0, tokens))
        else:
            for h in range(2):
                lines = slice(h * half, (h + 1) * half)
                rows[0, h, 0] = normalize(add(lines), final_gain_ref[...]).astype(jnp.bfloat16)
                for move in FIRST_SENDS:
                    if move[1] == h:
                        copies[move]().start()

    @pl.loop(1, PEERS)
    def _(q):
        target_copy(seen_from(q)).wait_recv()
    own_base = own * voc
    other_base = mirror * voc
    tile = voc // 2

    def stats_copy(q):
        there = seen_from(q)
        return remote(stats_out.at[q], stats_in.at[there], send_stats.at[q], recv_stats.at[there], at(peer(q)))

    @pl.loop(0, PEERS)
    def _(q):
        stats_out[q] = jnp.zeros(stats_out.shape[1:], jnp.float32)

    @pl.loop(0, len(SCHEDULE))
    def _(step):
        slot = looked_up([entry[0][0] for entry in SCHEDULE], step)
        h = looked_up([entry[0][1] for entry in SCHEDULE], step)
        for k, entry in enumerate(SCHEDULE):
            if len(entry) == 1:
                continue

            @pl.when(step == k)
            def _():
                for move in entry[1:]:
                    if len(move) == 2:
                        row_arrival(*move, 0).wait_recv()
                    else:
                        copies[move]().start()
        row_arrival(slot, h, 1).wait_recv()
        block = rows[slot, h].reshape(2 * half, width)
        wanted = jnp.concatenate([targets[2 * slot, pl.ds(h, 1), :], targets[2 * slot + 1, pl.ds(h, 1), :]], axis=1)
        high = total = hit = None
        for n in range(4):
            scores = lax.dot_general(vocab_t[n * tile:(n + 1) * tile, :], block, (((1,), (1,)), ((), ())), preferred_element_type=jnp.float32)
            base = (own_base if n < 2 else other_base) + n % 2 * tile
            match = lax.broadcasted_iota(jnp.int32, scores.shape, 0) == wanted - base
            stacked = scores.reshape(tile // 8, 8, 2 * half)
            found = jnp.sum(jnp.where(match, scores, 0.0).reshape(stacked.shape), axis=0)
            top = jnp.max(stacked, axis=0)
            if n:
                top = jnp.maximum(top, high)
            summed = jnp.sum(jnp.exp(stacked - top[None]), axis=0)
            if n:
                summed = summed + total * jnp.exp(high - top)
                found = found + hit
            high, total, hit = (top, summed, found)
        top = jnp.max(high, axis=0, keepdims=True)
        summed = jnp.sum(total * jnp.exp(high - top), axis=0, keepdims=True)
        found = jnp.sum(hit, axis=0, keepdims=True)
        for side in range(2):
            lanes = slice(side * half, (side + 1) * half)
            stats_out[2 * slot + side, pl.ds(h, 1), :] = top[:, lanes]
            stats_out[2 * slot + side, pl.ds(2 + h, 1), :] = summed[:, lanes]
            stats_out[2 * slot + side, pl.ds(4 + h, 1), :] = found[:, lanes]
        last = looked_up([int(all((e[0] != entry[0] and e[0][0] != entry[0][0] for e in SCHEDULE[k + 1:]))) for k, entry in enumerate(SCHEDULE)], step)

        @pl.when(last == 1)
        def _():

            @pl.when(slot > 0)
            def _():
                stats_copy(2 * slot).start()
            stats_copy(2 * slot + 1).start()
    stats_in[0] = stats_out[0]

    @pl.loop(1, PEERS)
    def _(q):
        stats_copy(seen_from(q)).wait_recv()
    every = stats_in[...]
    top = jnp.max(every[:, 0:2], axis=0)
    summed = jnp.sum(every[:, 2:4] * jnp.exp(every[:, 0:2] - top[None]), axis=0)
    found = jnp.sum(every[:, 4:6], axis=0)
    docs = docs_ref[...]
    two_rows = lax.broadcasted_iota(jnp.int32, docs.shape, 0)
    two_lanes = lax.broadcasted_iota(jnp.int32, docs.shape, 1)
    at_end = (two_rows == 1) & (two_lanes == half - 1) & (linear == devices - 1)
    counted = (targets[0, 2:4, :] == docs) & jnp.logical_not(at_end)
    token_loss = jnp.where(counted, top + jnp.log(summed) - found, 0.0)
    made_ref[0:2, :] = token_loss

    def whole(values):
        return jnp.sum(jnp.sum(values, axis=1, keepdims=True), axis=0, keepdims=True)

    def of_document(number):
        mask = docs == number
        return (whole(jnp.where(mask, token_loss, 0.0)), whole(jnp.where(mask, 1.0, 0.0)))
    lead_loss, lead_length = of_document(DOC_DEV * linear - 1)
    lines = lax.broadcasted_iota(jnp.int32, (8, 128), 0)
    sums_out[...] = jnp.where(lines == 0, whole(token_loss), jnp.where(lines == 1, lead_loss, jnp.where(lines == 2, lead_length, 0.0)))

    def sum_copy(q):
        there = seen_from(q)
        return remote(sums_out, sums_in.at[there], send_sums.at[q], recv_sums.at[there], at(peer(q)))

    def wide_copy(i):
        device, plane = across(i)
        return remote(wide_out, wide_in.at[i], send_wide.at[i], recv_wide.at[i], at(device, plane))

    def lead_copy():
        return remote(sums_out, lead_in, send_lead, recv_lead, shifted(-1))
    for q in range(1, PEERS):
        sum_copy(q).start()
    lead_copy().start()
    sums_in[0] = sums_out[...]
    parts = [of_document(DOC_DEV * linear + j) for j in range(DOC_DEV)]
    for q in range(1, PEERS):
        sum_copy(seen_from(q)).wait_recv()
    wide_out[...] = jnp.sum(sums_in[...], axis=0)
    for i in range(1, 2 * DP):
        wide_copy(i).start()
    wide_in[0] = wide_out[...]
    lead_copy().wait_recv()
    for i in range(1, 2 * DP):
        wide_copy(i).wait_recv()
    global_sum = jnp.sum(wide_in[...], axis=0)[0:1, 0:1]
    global_mean = global_sum / (tokens * devices - DOC_DEV * devices)
    lanes = lax.broadcasted_iota(jnp.int32, (1, 128), 1)
    scores = jnp.zeros((1, 128), jnp.float32)
    for j, (part_loss, part_length) in enumerate(parts):
        if j == DOC_DEV - 1:
            part_loss = part_loss + lead_in[1:2, 0:1]
            part_length = part_length + lead_in[2:3, 0:1]
        scores = jnp.where(lanes == j, part_loss / part_length - global_mean, scores)
    made_ref[2:3, :] = scores

    @pl.loop(1, OWNERS)
    def _(i):
        out(i).wait_send()
        back(i).wait_send()

    @pl.loop(1, PEERS)
    def _(q):
        target_copy(q).wait_send()
        stats_copy(q).wait_send()
    voc_across(0).wait_send()
    voc_across(1).wait_send()
    ids_copy().wait_send()
    lead_copy().wait_send()
    for q in range(1, PEERS):
        sum_copy(q).wait_send()
    for i in range(1, 2 * DP):
        wide_copy(i).wait_send()
    for dy in range(1, DP):
        voc_along(dy, dp).wait_send()
    for made in sends:
        made().wait_send()

def local(hidden_in, moe_gain, router_weight, expert_gate, expert_up, expert_down, final_gain, vocab_weight, token_ids, doc_ids, routes):
    tokens, width = hidden_in.shape
    here, _, hidden_units = expert_gate.shape
    voc = vocab_weight.shape[1]
    experts = OWNERS * here
    slots = max(2, 2 * TOP * tokens // experts)
    half = tokens // 2
    bf16, f32, i32 = (jnp.bfloat16, jnp.float32, jnp.int32)
    vmem = pl.BlockSpec(memory_space=pltpu.VMEM)
    hbm = pl.BlockSpec(memory_space=pl.ANY)
    dma = pltpu.SemaphoreType.DMA
    made = pl.pallas_call(kernel, out_shape=jax.ShapeDtypeStruct((8, half), f32), in_specs=[hbm] + [vmem] * 6 + [hbm] * 4, out_specs=vmem, scratch_shapes=[pltpu.VMEM((tokens, width), bf16), pltpu.VMEM((tokens, width), bf16), pltpu.VMEM((OWNERS, here, slots, width), bf16), pltpu.VMEM((here, OWNERS * slots, width), bf16), pltpu.VMEM((here, width, hidden_units), bf16), pltpu.VMEM((here, width, hidden_units), bf16), pltpu.VMEM((here, hidden_units, width), bf16), pltpu.VMEM((here, OWNERS * slots, width), bf16), pltpu.VMEM((OWNERS, here, slots, width), bf16), pltpu.VMEM((tokens, experts * slots), bf16), pltpu.VMEM((tokens, experts * slots), bf16), pltpu.VMEM((tokens, width), f32), pltpu.VMEM((width, voc), bf16), pltpu.VMEM((width, voc), bf16), pltpu.VMEM((2 * voc, width), bf16), pltpu.VMEM((8, 2, 2, half, width), bf16), pltpu.VMEM((8, half), i32), pltpu.VMEM((8, half), i32), pltpu.VMEM((PEERS, 8, half), i32), pltpu.VMEM((PEERS, 8, half), f32), pltpu.VMEM((PEERS, 8, half), f32), pltpu.VMEM((8, 128), f32), pltpu.VMEM((PEERS, 8, 128), f32), pltpu.VMEM((8, 128), f32), pltpu.VMEM((8, 128), f32), pltpu.VMEM((2 * DP, 8, 128), f32), dma((5,)), dma, dma((OWNERS,)), dma((OWNERS,)), dma((OWNERS,)), dma((OWNERS,)), dma((DP + 1,)), dma((DP + 1,)), dma, dma, dma((PEERS,)), dma((PEERS,)), dma((32,)), dma((32,)), dma((PEERS,)), dma((PEERS,)), dma((PEERS,)), dma((PEERS,)), dma, dma, dma((2 * DP,)), dma((2 * DP,))], compiler_params=pltpu.CompilerParams(collective_id=0, has_side_effects=True, vmem_limit_bytes=58 * 2 ** 20), name='scoring')(hidden_in, moe_gain.reshape(1, width), router_weight.T, routes.T, final_gain.reshape(1, width), token_ids.reshape(2, half), doc_ids.reshape(2, half), expert_gate, expert_up, expert_down, vocab_weight)
    return (made[0:2].reshape(tokens), made[2, :DOC_DEV])

def solution(mesh):
    in_specs = (P(BOTH, None), P(), P(), P('expert', None, None), P('expert', None, None), P('expert', None, None), P(), P(None, 'expert'), P(BOTH), P(BOTH), P(BOTH, None))
    return jax.shard_map(local, mesh=mesh, in_specs=in_specs, out_specs=(P(BOTH), P(BOTH)), check_vma=False)
```

time: 149 us -> 134 us (0.90)
  Pallas kernels: 146 us -> 131 us
    pallas_call x1, Pallas kernels: 146 us -> 131 us  [local(): pl.pallas_call(kernel, out_shape=jax.ShapeDtypeStruct((8, half), f32), in...]
    unnamed x2 -> x0, local copies, waits for them, and re-layouts: 2.36 us -> none
where the time goes in v3:
time: 134 us
  Pallas kernels  131 us (98%)
  local copies, waits for them, and re-layouts  2.44 us (2%)
    pallas_call x1, Pallas kernels, local(): pl.pallas_call(kernel, out_shape=jax.ShapeDtypeStruct((8, half), f32), in...  131 us

profile of v3, /device:TPU:1, one launch (start us, length us, event | category | flops | bytes accessed | tf_op | source)
XLA Modules:
  0.0 133.9 jit_solution(2921300921323735655)
XLA Ops:
  0.6 130.8 %scoring.1 = f32[8,128]{1,0:T(8,128)} custom-call(bf16[256,1024]{1,0:T(8,128)(2,1)} %hidden_hbm.1, f32[1,1024]{1,0:T(1,128)} %bitcast.11, bf16[64,1024]{1,0:T(8,128)(2,1)} %bitcast.10, s32[2,256]{1,0:T(2,128)} %bitcast.13, f32[1,1024]{1,0:T(1,128)} %bitcast.12, s32[2,128]{1,0:T(2,128)} %bitcast.14, s32[2,128]{1,0:T(2,128)} %bitcast.15, ...), custom_call_target="tpu_custom_call" | custom-call | tf_op jit(solution)/shard_map/scoring/pallas_call | solution.py:457
  131.5 1.2 slice_bitcast_fusion.1
  132.7 1.2 slice_bitcast_fusion

commit v4 on v3

--- a/solution.py
+++ b/solution.py
@@ -35,6 +35,13 @@
     ((5, 1),),
 )
 EPSILON = 1e-06
+
+def each(low, high):
+
+    def over(body):
+        for i in range(low, high):
+            body(i)
+    return over
 MESH_ID = pl.DeviceIdType.MESH
 EPSILON = 1e-06
 
@@ -73,15 +80,21 @@
     def shifted(steps):
         other = (linear + steps + devices) % devices
         return at(other % OWNERS, other // OWNERS)
+    x_part = [(x + d) % SIDE * 8 for d in range(SIDE)]
+    z_part = [(z + d) % SIDE * 2 for d in range(SIDE)]
+    c_part = [core, 1 - core]
 
     def partner(i, sign):
-        dx = i % 8 // 2
-        dz = (i // 8 + SIDE - dx) % SIDE
-        dc = i % 2
+        dx, dc, k = (i % 4, i // 16, i // 4 % 4)
+        dz = (k + SIDE - dx) % SIDE
+        if isinstance(i, int):
+            return x_part[sign * dx % SIDE] + z_part[sign * dz % SIDE] + c_part[dc]
         return (x + sign * dx + SIDE) % SIDE * 8 + (z + sign * dz + SIDE) % SIDE * 2 + (core + dc) % 2
 
     def peer(q):
         jx, jz, jc = (q // 8, q // 2 % SIDE, q % 2)
+        if isinstance(q, int):
+            return (mate_x if jx else x) * 8 + z_part[jz] + c_part[jc]
         return (x + jx * (mate_x - x)) * 8 + (z + jz) % SIDE * 2 + (core + jc) % 2
 
     def seen_from(q):
@@ -94,7 +107,7 @@
         return pltpu.make_async_remote_copy(src_ref=source, dst_ref=target, send_sem=send, recv_sem=recv, device_id=device, device_id_type=MESH_ID)
     barrier = pltpu.get_barrier_semaphore()
 
-    @pl.loop(1, OWNERS)
+    @each(1, OWNERS)
     def _(i):
         pl.semaphore_signal(barrier, inc=1, device_id=at(partner(i, 1)), device_id_type=MESH_ID)
     for i in range(2, 2 * DP):
@@ -144,14 +157,15 @@
         dx = (owner // 8 + SIDE - x) % SIDE
         dz = (owner // 2 % SIDE + SIDE - z) % SIDE
         dc = (owner + core) % 2
-        index = (dx + dz) % SIDE * 8 + dx * 2 + dc
+        k = (dx + dz) % SIDE
+        index = dc * 16 + k * 4 + dx
         own_rank = jnp.sum(jnp.where(chosen, rank, 0.0), axis=0, keepdims=True).astype(jnp.int32)
         return index * part + expert % local * slots + own_rank
     first_pos = position(first, is_first)
     second_pos = position(second, is_second)
 
     def slot_rows(i):
-        return pl.ds(pl.multiple_of(i * slots, slots), slots)
+        return pl.ds(i * slots if isinstance(i, int) else pl.multiple_of(i * slots, slots), slots)
 
     def out(i):
         return remote(outgoing.at[i], arrived.at[:, slot_rows(i)], send_out.at[i], recv_out.at[i], at(partner(i, 1)))
@@ -167,7 +181,7 @@
             own_copy = pltpu.make_async_copy(outgoing.at[0], arrived.at[:, pl.ds(0, slots)], self_sem)
             own_copy.start()
 
-        @pl.loop(max(1, group * per_group), (group + 1) * per_group)
+        @each(max(1, group * per_group), (group + 1) * per_group)
         def _(i):
             out(i).start()
     ids_copy().wait_recv()
@@ -186,7 +200,7 @@
         there = seen_from(q)
         return remote(targets.at[0], targets.at[there], send_tgt.at[q], recv_tgt.at[there], at(peer(q)))
 
-    @pl.loop(1, PEERS)
+    @each(1, PEERS)
     def _(q):
         target_copy(q).start()
     router_scores = lax.dot_general(router_ref[...], normed[...], (((1,), (1,)), ((), ())), preferred_element_type=jnp.float32)
@@ -216,7 +230,7 @@
     for group in range(GROUPS):
         low, high = (max(1, group * per_group), (group + 1) * per_group)
 
-        @pl.loop(low, high)
+        @each(low, high)
         def _(i):
             out(i).wait_recv()
 
@@ -231,7 +245,7 @@
             home = pltpu.make_async_copy(result.at[:, pl.ds(0, slots)], returned.at[0], self_sem)
             home.start()
 
-        @pl.loop(low, high)
+        @each(low, high)
         def _(i):
             back(i).start()
     for dy in range(DP):
@@ -276,7 +290,7 @@
     for group in range(GROUPS):
         low, high = (max(1, group * per_group), (group + 1) * per_group)
 
-        @pl.loop(low, high)
+        @each(low, high)
         def _(i):
             back(i).wait_recv()
         block = returned[pl.ds(group * per_group, per_group)].reshape(per_group * part, width)
@@ -294,12 +308,12 @@
                     if move[1] == h:
                         copies[move]().start()
 
-    @pl.loop(1, PEERS)
+    @each(1, PEERS)
     def _(q):
         target_copy(seen_from(q)).wait_recv()
     own_base = own * voc
     other_base = mirror * voc
-    tile = voc // 2
+    tile = voc
 
     def stats_copy(q):
         there = seen_from(q)
@@ -328,9 +342,9 @@
         block = rows[slot, h].reshape(2 * half, width)
         wanted = jnp.concatenate([targets[2 * slot, pl.ds(h, 1), :], targets[2 * slot + 1, pl.ds(h, 1), :]], axis=1)
         high = total = hit = None
-        for n in range(4):
+        for n in range(2):
             scores = lax.dot_general(vocab_t[n * tile:(n + 1) * tile, :], block, (((1,), (1,)), ((), ())), preferred_element_type=jnp.float32)
-            base = (own_base if n < 2 else other_base) + n % 2 * tile
+            base = own_base if n == 0 else other_base
             match = lax.broadcasted_iota(jnp.int32, scores.shape, 0) == wanted - base
             stacked = scores.reshape(tile // 8, 8, 2 * half)
             found = jnp.sum(jnp.where(match, scores, 0.0).reshape(stacked.shape), axis=0)
@@ -361,7 +375,7 @@
             stats_copy(2 * slot + 1).start()
     stats_in[0] = stats_out[0]
 
-    @pl.loop(1, PEERS)
+    @each(1, PEERS)
     def _(q):
         stats_copy(seen_from(q)).wait_recv()
     every = stats_in[...]
@@ -421,12 +435,12 @@
         scores = jnp.where(lanes == j, part_loss / part_length - global_mean, scores)
     made_ref[2:3, :] = scores
 
-    @pl.loop(1, OWNERS)
+    @each(1, OWNERS)
     def _(i):
         out(i).wait_send()
         back(i).wait_send()
 
-    @pl.loop(1, PEERS)
+    @each(1, PEERS)
     def _(q):
         target_copy(q).wait_send()
         stats_copy(q).wait_send()

time: 134 us -> 129 us (0.963)
  Pallas kernels: 131 us -> 126 us
    pallas_call x1, Pallas kernels: 131 us -> 126 us  [local(): pl.pallas_call(kernel, out_shape=jax.ShapeDtypeStruct((8, half), f32), in...]
where the time goes in v4:
time: 129 us
  Pallas kernels  126 us (98%)
  local copies, waits for them, and re-layouts  2.44 us (2%)
    pallas_call x1, Pallas kernels, local(): pl.pallas_call(kernel, out_shape=jax.ShapeDtypeStruct((8, half), f32), in...  126 us

profile of v4, /device:TPU:1, one launch (start us, length us, event | category | flops | bytes accessed | tf_op | source)
XLA Modules:
  0.0 128.8 jit_solution(11650178525930628916)
XLA Ops:
  0.6 125.7 %scoring.1 = f32[8,128]{1,0:T(8,128)} custom-call(bf16[256,1024]{1,0:T(8,128)(2,1)} %hidden_hbm.1, f32[1,1024]{1,0:T(1,128)} %bitcast.11, bf16[64,1024]{1,0:T(8,128)(2,1)} %bitcast.10, s32[2,256]{1,0:T(2,128)} %bitcast.13, f32[1,1024]{1,0:T(1,128)} %bitcast.12, s32[2,128]{1,0:T(2,128)} %bitcast.14, s32[2,128]{1,0:T(2,128)} %bitcast.15, ...), custom_call_target="tpu_custom_call" | custom-call | tf_op jit(solution)/shard_map/scoring/pallas_call | solution.py:471
  126.3 1.2 slice_bitcast_fusion.1
  127.5 1.2 slice_bitcast_fusion

commit v5 on v4

--- a/solution.py
+++ b/solution.py
@@ -286,6 +286,13 @@
         else:
             copies[slot, h, way] = row_copy(slot, h, slot, sibling, 1)
     home.wait()
+    for i in range(1, OWNERS):
+        out(i).wait_send()
+    for q in range(1, PEERS):
+        target_copy(q).wait_send()
+    voc_across(0).wait_send()
+    voc_across(1).wait_send()
+    ids_copy().wait_send()
     mixed[...] = hidden[...].astype(jnp.float32)
     for group in range(GROUPS):
         low, high = (max(1, group * per_group), (group + 1) * per_group)
@@ -415,12 +422,20 @@
     lead_copy().start()
     sums_in[0] = sums_out[...]
     parts = [of_document(DOC_DEV * linear + j) for j in range(DOC_DEV)]
+    for i in range(1, OWNERS):
+        back(i).wait_send()
+    for dy in range(1, DP):
+        voc_along(dy, dp).wait_send()
     for q in range(1, PEERS):
         sum_copy(seen_from(q)).wait_recv()
     wide_out[...] = jnp.sum(sums_in[...], axis=0)
     for i in range(1, 2 * DP):
         wide_copy(i).start()
     wide_in[0] = wide_out[...]
+    for made in sends:
+        made().wait_send()
+    for q in range(1, PEERS):
+        stats_copy(q).wait_send()
     lead_copy().wait_recv()
     for i in range(1, 2 * DP):
         wide_copy(i).wait_recv()
@@ -434,28 +449,12 @@
             part_length = part_length + lead_in[2:3, 0:1]
         scores = jnp.where(lanes == j, part_loss / part_length - global_mean, scores)
     made_ref[2:3, :] = scores
-
-    @each(1, OWNERS)
-    def _(i):
-        out(i).wait_send()
-        back(i).wait_send()
-
-    @each(1, PEERS)
-    def _(q):
-        target_copy(q).wait_send()
-        stats_copy(q).wait_send()
-    voc_across(0).wait_send()
-    voc_across(1).wait_send()
-    ids_copy().wait_send()
-    lead_copy().wait_send()
     for q in range(1, PEERS):
         sum_copy(q).wait_send()
     for i in range(1, 2 * DP):
         wide_copy(i).wait_send()
-    for dy in range(1, DP):
-        voc_along(dy, dp).wait_send()
-    for made in sends:
-        made().wait_send()
+    lead_copy().wait_send()
+
 
 def local(hidden_in, moe_gain, router_weight, expert_gate, expert_up, expert_down, final_gain, vocab_weight, token_ids, doc_ids, routes):
     tokens, width = hidden_in.shape

time: 129 us -> 129 us (level)
  no operation moved by 1% of the time
where the time goes in v5:
time: 129 us
  Pallas kernels  125 us (97%)
  local copies, waits for them, and re-layouts  2.44 us (2%)
    pallas_call x1, Pallas kernels, local(): pl.pallas_call(kernel, out_shape=jax.ShapeDtypeStruct((8, half), f32), in...  125 us

profile of v5, /device:TPU:1, one launch (start us, length us, event | category | flops | bytes accessed | tf_op | source)
XLA Modules:
  0.0 128.6 jit_solution(13585359970356549190)
XLA Ops:
  0.6 125.5 %scoring.1 = f32[8,128]{1,0:T(8,128)} custom-call(bf16[256,1024]{1,0:T(8,128)(2,1)} %hidden_hbm.1, f32[1,1024]{1,0:T(1,128)} %bitcast.11, bf16[64,1024]{1,0:T(8,128)(2,1)} %bitcast.10, s32[2,256]{1,0:T(2,128)} %bitcast.13, f32[1,1024]{1,0:T(1,128)} %bitcast.12, s32[2,128]{1,0:T(2,128)} %bitcast.14, s32[2,128]{1,0:T(2,128)} %bitcast.15, ...), custom_call_target="tpu_custom_call" | custom-call | tf_op jit(solution)/shard_map/scoring/pallas_call | solution.py:470
  126.1 1.2 slice_bitcast_fusion.1
  127.3 1.2 slice_bitcast_fusion
